TPU v7x, 32 devices: a whole 2x2x4 slice. The times are simulated.
32 devices in a mesh: dp: 16 (over z, x, core), tensor: 2 (over y).
Axes of the slice: x: 2, y: 2, z: 4, core: 2. Of those that a mesh axis runs over, the one named last changes fastest.
Arguments:
- hidden_in: bfloat16 [16384, 1024], P(('dp', 'tensor')), may hold values from -6 to 6
- positions: int32 [16384], P('dp'), may hold values from 0 to 1023, as said below
- gain_attention: float32 [1024], replicated, may hold values from 0.1 to 1.9
- gain_feedforward: float32 [1024], replicated, may hold values from 0.1 to 1.9
- gain_query: float32 [128], replicated, may hold values from 0.7 to 5
- gain_key: float32 [128], replicated, may hold values from 0.7 to 5
- query_proj: bfloat16 [1024, 2048], P('dp', 'tensor'), may hold values from -0.1875 to 0.1875
- key_proj: bfloat16 [1024, 1024], P('dp', 'tensor'), may hold values from -0.1875 to 0.1875
- value_proj: bfloat16 [1024, 1024], P('dp', 'tensor'), may hold values from -0.1875 to 0.1875
- out_proj: bfloat16 [2048, 1024], P(('tensor', 'dp')), may hold values from -3 to 3
- gate_proj: bfloat16 [1024, 3072], P('dp', 'tensor'), may hold values from -0.1875 to 0.1875
- up_proj: bfloat16 [1024, 3072], P('dp', 'tensor'), may hold values from -0.1875 to 0.1875
- down_proj: bfloat16 [3072, 1024], P(('tensor', 'dp')), may hold values from -0.21875 to 0.21875
- cotangent: bfloat16 [16384, 1024], P(('dp', 'tensor')), may hold values from -6 to 6
Outputs:
- hidden_out: bfloat16 [16384, 1024], P(('dp', 'tensor'))
- grad_hidden: float32 [16384, 1024], P(('dp', 'tensor'))
- attention_gain_grad: float32 [1024], replicated
- feedforward_gain_grad: float32 [1024], replicated
- query_gain_grad: float32 [128], replicated
- key_gain_grad: float32 [128], replicated
- query_grads: float32 [1024, 2048], P('dp', 'tensor')
- key_grads: float32 [1024, 1024], P('dp', 'tensor')
- value_grads: float32 [1024, 1024], P('dp', 'tensor')
- out_grads: float32 [2048, 1024], P(('tensor', 'dp'))
- gate_grads: float32 [1024, 3072], P('dp', 'tensor')
- up_grads: float32 [1024, 3072], P('dp', 'tensor')
- down_grads: float32 [3072, 1024], P(('tensor', 'dp'))
Inputs may be any that keep to these rules, and one draw needn't show every extreme that they name: Within each sequence of 1024 tokens the positions start at 0 and rise by one from token to token, except that they restart at 0 where a document begins; some sequence holds one document.
All inputs are finite; a program needn't handle non-finite values.
Results may differ from a plain program's by a relative error of at most 0.02.
The roundings to bfloat16 on the way count: a program that leaves them out, or rounds other values in their place, can miss the bound.
Values may be sent and summed in bfloat16 or wider, within the bound.
No kernel may reach another device: no remote copies, remote signals or barrier semaphores. Data moves between devices by JAX's collectives and lax.ppermute only.
A program may use at most 256 MiB of HBM per device.

v0:
```python
import math

import jax
import jax.numpy as jnp
from jax import lax
from jax.sharding import PartitionSpec as P

HD = 128


EPS = 1e-06
THETA = 1000000.0


def rotary_tables(positions, width):
    half_width = width // 2
    freq_index = jnp.arange(half_width).astype(jnp.float32)
    inverse_freq = jnp.exp(freq_index * (-2.0 * math.log(THETA) / width))
    angles = positions.astype(jnp.float32)[:, None] * inverse_freq[None, :]
    return (jnp.cos(angles)[:, None, :], jnp.sin(angles)[:, None, :])


def rotate(values, cosine_table, sine_table):
    half_width = values.shape[-1] // 2
    lower_half = values[..., :half_width]
    upper_half = values[..., half_width:]
    return jnp.concatenate(
        (
            lower_half * cosine_table - upper_half * sine_table,
            upper_half * cosine_table + lower_half * sine_table,
        ),
        -1,
    )


def rotate_back(grad_values, cosine_table, sine_table):
    half_width = grad_values.shape[-1] // 2
    lower_half = grad_values[..., :half_width]
    upper_half = grad_values[..., half_width:]
    return jnp.concatenate(
        (
            lower_half * cosine_table + upper_half * sine_table,
            upper_half * cosine_table - lower_half * sine_table,
        ),
        -1,
    )


def rms_unit(values):
    inv_scale = lax.rsqrt(jnp.mean(values * values, -1, keepdims=True) + EPS)
    return (values * inv_scale, inv_scale)


def rms_back(grad_out, gain_vec, unit_vals, inv_scale):
    scaled_grad = grad_out * gain_vec
    return inv_scale * (
        scaled_grad - unit_vals * jnp.mean(scaled_grad * unit_vals, -1, keepdims=True)
    )


def contract_rows(left, right):
    return lax.dot_general(
        left, right, (((0,), (0,)), ((), ())), preferred_element_type=jnp.float32
    )


def contract_cols(left, right):
    return lax.dot_general(
        left, right, (((1,), (1,)), ((), ())), preferred_element_type=jnp.float32
    )


def attend(query_b, key_b, value_b):
    length = query_b.shape[0]
    block_rows = min(length, 512)
    block_count = length // block_rows
    scale_qk = 1.0 / math.sqrt(query_b.shape[-1])
    outputs = []
    log_sums = []
    for block in range(block_count):
        row_start = block * block_rows
        key_end = row_start + block_rows
        query_block = query_b[row_start:key_end]
        scores = (
            jnp.einsum(
                "qgrd,kgd->grqk", query_block, key_b[:key_end], preferred_element_type=jnp.float32
            )
            * scale_qk
        )
        causal = (row_start + jnp.arange(block_rows, dtype=jnp.int32))[:, None] >= jnp.arange(
            key_end, dtype=jnp.int32
        )[None, :]
        scores = jnp.where(causal, scores, -jnp.inf)
        top_score = jnp.max(scores, -1, keepdims=True)
        shifted = jnp.exp(scores - top_score)
        sum_exp = jnp.sum(shifted, -1, keepdims=True)
        probs_b = (shifted / sum_exp).astype(jnp.bfloat16)
        outputs.append(
            jnp.einsum(
                "grqk,kgd->qgrd", probs_b, value_b[:key_end], preferred_element_type=jnp.float32
            )
        )
        log_sums.append(top_score + jnp.log(sum_exp))
    return (jnp.concatenate(outputs, 0), log_sums)


def attend_back(query_b, key_b, value_b, grad_b, log_sums):
    length = query_b.shape[0]
    block_rows = min(length, 512)
    block_count = length // block_rows
    scale_qk = 1.0 / math.sqrt(query_b.shape[-1])
    key_acc = jnp.zeros(key_b.shape, jnp.float32)
    value_acc = jnp.zeros(key_b.shape, jnp.float32)
    grad_queries = []
    for block in range(block_count):
        row_start = block * block_rows
        key_end = row_start + block_rows
        query_block = query_b[row_start:key_end]
        grad_block = grad_b[row_start:key_end]
        keys_seen = key_b[:key_end]
        scores = (
            jnp.einsum("qgrd,kgd->grqk", query_block, keys_seen, preferred_element_type=jnp.float32)
            * scale_qk
        )
        causal = (row_start + jnp.arange(block_rows, dtype=jnp.int32))[:, None] >= jnp.arange(
            key_end, dtype=jnp.int32
        )[None, :]
        scores = jnp.where(causal, scores, -jnp.inf)
        probs = jnp.exp(scores - log_sums[block])
        probs_b = probs.astype(jnp.bfloat16)
        grad_probs = jnp.einsum(
            "qgrd,kgd->grqk", grad_block, value_b[:key_end], preferred_element_type=jnp.float32
        )
        row_dot = jnp.sum(probs * grad_probs, -1, keepdims=True)
        grad_scores_b = (probs * (grad_probs - row_dot)).astype(jnp.bfloat16)
        grad_queries.append(
            jnp.einsum(
                "grqk,kgd->qgrd", grad_scores_b, keys_seen, preferred_element_type=jnp.float32
            )
            * scale_qk
        )
        key_acc = key_acc.at[:key_end].add(
            jnp.einsum(
                "grqk,qgrd->kgd", grad_scores_b, query_block, preferred_element_type=jnp.float32
            )
            * scale_qk
        )
        value_acc = value_acc.at[:key_end].add(
            jnp.einsum("grqk,qgrd->kgd", probs_b, grad_block, preferred_element_type=jnp.float32)
        )
    return (jnp.concatenate(grad_queries, 0), key_acc, value_acc)


def local(
    hidden_in,
    positions,
    gain_attention,
    gain_feedforward,
    gain_query,
    gain_key,
    query_proj,
    key_proj,
    value_proj,
    out_proj,
    gate_proj,
    up_proj,
    down_proj,
    cotangent,
):
    length = positions.shape[0]
    heads_here = query_proj.shape[1] // HD
    groups_here = key_proj.shape[1] // HD
    width_query = heads_here * HD
    width_key = groups_here * HD
    full_query, full_key, full_value, full_out, full_gate, full_up, full_down = (
        lax.all_gather(query_proj, "dp", axis=0, tiled=True),
        lax.all_gather(key_proj, "dp", axis=0, tiled=True),
        lax.all_gather(value_proj, "dp", axis=0, tiled=True),
        lax.all_gather(out_proj, "dp", axis=0, tiled=True),
        lax.all_gather(gate_proj, "dp", axis=0, tiled=True),
        lax.all_gather(up_proj, "dp", axis=0, tiled=True),
        lax.all_gather(down_proj, "dp", axis=0, tiled=True),
    )
    proj_qkv = jnp.concatenate((full_query, full_key, full_value), 1)
    cosine_table, sine_table = rotary_tables(positions, HD)
    hidden_f = hidden_in.astype(jnp.float32)
    unit_attn, scale_attn = rms_unit(hidden_f)
    normed_attn = (unit_attn * gain_attention).astype(jnp.bfloat16)
    rows_attn = lax.all_gather(normed_attn, "tensor", axis=0, tiled=True)
    projected = jnp.dot(rows_attn, proj_qkv, preferred_element_type=jnp.float32)
    query_raw = projected[:, :width_query].reshape(length, heads_here, HD)
    key_raw = projected[:, width_query : width_query + width_key].reshape(length, groups_here, HD)
    value_b = (
        projected[:, width_query + width_key :]
        .astype(jnp.bfloat16)
        .reshape(length, groups_here, HD)
    )
    query_unit, query_scale = rms_unit(query_raw)
    key_unit, key_scale = rms_unit(key_raw)
    query_b = (
        rotate(query_unit * gain_query, cosine_table, sine_table)
        .astype(jnp.bfloat16)
        .reshape(length, groups_here, heads_here // groups_here, HD)
    )
    key_b = rotate(key_unit * gain_key, cosine_table, sine_table).astype(jnp.bfloat16)
    heads_out, log_sums = attend(query_b, key_b, value_b)
    heads_b = heads_out.reshape(length, width_query).astype(jnp.bfloat16)
    resid = hidden_f + lax.psum_scatter(
        jnp.dot(heads_b, full_out, preferred_element_type=jnp.float32),
        "tensor",
        scatter_dimension=0,
        tiled=True,
    )
    unit_mlp, scale_mlp = rms_unit(resid)
    normed_mlp = (unit_mlp * gain_feedforward).astype(jnp.bfloat16)
    rows_mlp = lax.all_gather(normed_mlp, "tensor", axis=0, tiled=True)
    gate_val = jnp.dot(rows_mlp, full_gate, preferred_element_type=jnp.float32)
    up_val = jnp.dot(rows_mlp, full_up, preferred_element_type=jnp.float32)
    sigmoid_gate = jax.nn.sigmoid(gate_val)
    active_b = (gate_val * sigmoid_gate * up_val).astype(jnp.bfloat16)
    output_b = (
        resid
        + lax.psum_scatter(
            jnp.dot(active_b, full_down, preferred_element_type=jnp.float32).astype(jnp.bfloat16),
            "tensor",
            scatter_dimension=0,
            tiled=True,
        ).astype(jnp.float32)
    ).astype(jnp.bfloat16)
    rows_cot = lax.all_gather(cotangent, "tensor", axis=0, tiled=True)
    grad_down = contract_rows(active_b, rows_cot)
    grad_active = contract_cols(rows_cot, full_down)
    grad_gate_b = (
        grad_active * up_val * sigmoid_gate * (1.0 + gate_val * (1.0 - sigmoid_gate))
    ).astype(jnp.bfloat16)
    grad_up_b = (grad_active * gate_val * sigmoid_gate).astype(jnp.bfloat16)
    grad_gate = contract_rows(rows_mlp, grad_gate_b)
    grad_up = contract_rows(rows_mlp, grad_up_b)
    gate_part = contract_cols(grad_gate_b, full_gate)
    grad_normed_mlp = lax.psum_scatter(
        (gate_part + contract_cols(grad_up_b, full_up)).astype(jnp.bfloat16),
        "tensor",
        scatter_dimension=0,
        tiled=True,
    ).astype(jnp.float32)
    term_feedforward = jnp.sum(grad_normed_mlp * unit_mlp, 0)
    grad_resid = cotangent.astype(jnp.float32) + rms_back(
        grad_normed_mlp, gain_feedforward, unit_mlp, scale_mlp
    )
    grad_resid_b = grad_resid.astype(jnp.bfloat16)
    rows_resid = lax.all_gather(grad_resid_b, "tensor", axis=0, tiled=True)
    grad_out = contract_rows(heads_b, rows_resid)
    grad_heads_b = (
        contract_cols(rows_resid, full_out)
        .astype(jnp.bfloat16)
        .reshape(length, groups_here, heads_here // groups_here, HD)
    )
    grad_qrot, grad_krot, grad_value = attend_back(query_b, key_b, value_b, grad_heads_b, log_sums)
    grad_qnormed = rotate_back(grad_qrot.reshape(length, heads_here, HD), cosine_table, sine_table)
    grad_knormed = rotate_back(grad_krot, cosine_table, sine_table)
    term_query = jnp.sum(grad_qnormed * query_unit, (0, 1))
    term_key = jnp.sum(grad_knormed * key_unit, (0, 1))
    grad_qkv_b = jnp.concatenate(
        (
            rms_back(grad_qnormed, gain_query, query_unit, query_scale).reshape(
                length, width_query
            ),
            rms_back(grad_knormed, gain_key, key_unit, key_scale).reshape(length, width_key),
            grad_value.reshape(length, width_key),
        ),
        1,
    ).astype(jnp.bfloat16)
    grad_qkv = contract_rows(rows_attn, grad_qkv_b)
    grad_normed_attn = lax.psum_scatter(
        contract_cols(grad_qkv_b, proj_qkv).astype(jnp.bfloat16),
        "tensor",
        scatter_dimension=0,
        tiled=True,
    ).astype(jnp.float32)
    term_attention = jnp.sum(grad_normed_attn * unit_attn, 0)
    grad_hidden = grad_resid + rms_back(grad_normed_attn, gain_attention, unit_attn, scale_attn)
    sum_attention, sum_feedforward, sum_query, sum_key = lax.psum(
        (term_attention, term_feedforward, term_query, term_key), ("dp", "tensor")
    )
    grad_query_w = grad_qkv[:, :width_query]
    grad_key_w = grad_qkv[:, width_query : width_query + width_key]
    grad_value_w = grad_qkv[:, width_query + width_key :]
    sent_query, sent_key, sent_value, sent_out, sent_gate, sent_up, sent_down = (
        lax.psum_scatter(
            grad_query_w.astype(jnp.bfloat16), "dp", scatter_dimension=0, tiled=True
        ).astype(jnp.float32),
        lax.psum_scatter(
            grad_key_w.astype(jnp.bfloat16), "dp", scatter_dimension=0, tiled=True
        ).astype(jnp.float32),
        lax.psum_scatter(
            grad_value_w.astype(jnp.bfloat16), "dp", scatter_dimension=0, tiled=True
        ).astype(jnp.float32),
        lax.psum_scatter(
            grad_out.astype(jnp.bfloat16), "dp", scatter_dimension=0, tiled=True
        ).astype(jnp.float32),
        lax.psum_scatter(
            grad_gate.astype(jnp.bfloat16), "dp", scatter_dimension=0, tiled=True
        ).astype(jnp.float32),
        lax.psum_scatter(
            grad_up.astype(jnp.bfloat16), "dp", scatter_dimension=0, tiled=True
        ).astype(jnp.float32),
        lax.psum_scatter(
            grad_down.astype(jnp.bfloat16), "dp", scatter_dimension=0, tiled=True
        ).astype(jnp.float32),
    )
    return (
        output_b,
        grad_hidden,
        sum_attention,
        sum_feedforward,
        sum_query,
        sum_key,
        sent_query,
        sent_key,
        sent_value,
        sent_out,
        sent_gate,
        sent_up,
        sent_down,
    )


def solution(mesh):
    placed = (
        P(("dp", "tensor"), None),
        P("dp"),
        P(),
        P(),
        P(),
        P(),
        P("dp", "tensor"),
        P("dp", "tensor"),
        P("dp", "tensor"),
        P(("tensor", "dp"), None),
        P("dp", "tensor"),
        P("dp", "tensor"),
        P(("tensor", "dp"), None),
        P(("dp", "tensor"), None),
    )
    return jax.shard_map(
        local,
        mesh=mesh,
        in_specs=placed,
        out_specs=(
            P(("dp", "tensor"), None),
            P(("dp", "tensor"), None),
            P(),
            P(),
            P(),
            P(),
            P("dp", "tensor"),
            P("dp", "tensor"),
            P("dp", "tensor"),
            P(("tensor", "dp"), None),
            P("dp", "tensor"),
            P("dp", "tensor"),
            P(("tensor", "dp"), None),
        ),
        check_vma=False,
    )
```

profile of v0, /device:TPU:0, one launch (start us, length us, event | category | flops | bytes accessed | tf_op | source)
XLA Modules:
  0.0 1142.5 jit_solution(466899385736626005)
XLA Ops:
  18.0 36.4 %all-gather.14.cloned.1.call-done = bf16[1024,1024]{1,0:T(8,128)(2,1)} async-done(((bf16[64,1024]{1,0:T(8,128)(2,1)}), bf16[1024,1024]{1,0:T(8,128)(2,1)}) %all-gather.14.cloned.1.call-update) | async-done | bytes 2097168 | tf_op jit(solution)/shard_map/all_gather | solution.py:176
  57.5 35.7 %all-gather.16.cloned.1.call-done = bf16[1024,512]{1,0:T(8,128)(2,1)} async-done(((bf16[64,512]{1,0:T(8,128)(2,1)}), bf16[1024,512]{1,0:T(8,128)(2,1)}) %all-gather.16.cloned.1.call-update) | async-done | bytes 1048592 | tf_op jit(solution)/shard_map/all_gather | solution.py:177
  95.4 36.7 %all-gather.18.cloned.1.call-done = bf16[1024,512]{1,0:T(8,128)(2,1)} async-done(((bf16[64,512]{1,0:T(8,128)(2,1)}), bf16[1024,512]{1,0:T(8,128)(2,1)}) %all-gather.18.cloned.1.call-update) | async-done | bytes 1048592 | tf_op jit(solution)/shard_map/all_gather | solution.py:178
  134.5 31.8 %all-gather.12.cloned.1.call-done = bf16[1024,1024]{1,0:T(8,128)(2,1)} async-done(((bf16[512,1024]{1,0:T(8,128)(2,1)}), bf16[1024,1024]{1,0:T(8,128)(2,1)}) %all-gather.12.cloned.1.call-update) | async-done | bytes 2097168 | tf_op jit(solution)/shard_map/all_gather | solution.py:189
  166.2 7.4 fusion.80
  193.4 3.6 multiply_reduce_fusion.4
  206.3 9.0 fusion.79
  215.3 8.0 fusion.3
  238.4 6.8 fusion.82
  246.3 53.8 %reduce-scatter.12.cloned.1.call-done = f32[512,1024]{1,0:T(8,128)} async-done(((f32[1024,1024]{1,0:T(8,128)}), f32[512,1024]{1,0:T(8,128)}) %reduce-scatter.12.cloned.1.call-update) | async-done | bytes 2097168 | tf_op jit(solution)/shard_map/reduce_scatter | solution.py:208
  305.5 42.3 %all-gather.24.cloned.1.call-done = bf16[1024,1536]{1,0:T(8,128)(2,1)} async-done(((bf16[64,1536]{1,0:T(8,128)(2,1)}), bf16[1024,1536]{1,0:T(8,128)(2,1)}) %all-gather.24.cloned.1.call-update) | async-done | bytes 3145744 | tf_op jit(solution)/shard_map/all_gather | solution.py:180
  347.8 33.6 %all-gather.22.cloned.1.call-done = bf16[1024,1024]{1,0:T(8,128)(2,1)} async-done(((bf16[512,1024]{1,0:T(8,128)(2,1)}), bf16[1024,1024]{1,0:T(8,128)(2,1)}) %all-gather.22.cloned.1.call-update) | async-done | bytes 2097168 | tf_op jit(solution)/shard_map/all_gather | solution.py:216
  381.4 8.6 fusion.83
  390.0 39.2 %all-gather.26.cloned.1.call-done = bf16[1024,1536]{1,0:T(8,128)(2,1)} async-done(((bf16[64,1536]{1,0:T(8,128)(2,1)}), bf16[1024,1536]{1,0:T(8,128)(2,1)}) %all-gather.26.cloned.1.call-update) | async-done | bytes 3145744 | tf_op jit(solution)/shard_map/all_gather | solution.py:181
  429.2 8.6 fusion.84
  437.8 24.3 %all-gather.30.cloned.1.call-done = bf16[1024,1024]{1,0:T(8,128)(2,1)} async-done(((bf16[512,1024]{1,0:T(8,128)(2,1)}), bf16[1024,1024]{1,0:T(8,128)(2,1)}) %all-gather.30.cloned.1.call-update) | async-done | bytes 2097168 | tf_op jit(solution)/shard_map/all_gather | solution.py:230
  462.1 47.8 %all-gather.28.cloned.1.call-done = bf16[1536,1024]{1,0:T(8,128)(2,1)} async-done(((bf16[96,1024]{1,0:T(8,128)(2,1)}), bf16[1536,1024]{1,0:T(8,128)(2,1)}) %all-gather.28.cloned.1.call-update) | async-done | bytes 3145744 | tf_op jit(solution)/shard_map/all_gather | solution.py:182
  509.9 11.8 %multiply_convert_fusion = (bf16[1024,1536]{1,0:T(8,128)(2,1)S(1)}, bf16[1024,1536]{1,0:T(8,128)(2,1)S(1)}, bf16[1024,1536]{1,0:T(8,128)(2,1)}) fusion(f32[1024,1536]{1,0:T(8,128)} %fusion.83, f32[1024,1536]{1,0:T(8,128)} %fusion.84, bf16[1024,1024]{1,0:T(8,128)(2,1)} %all-gather.30.cloned.1.call-done, bf16[1536,1024]{1,0:T(8,128)(2,1)} %all-gather.28.cloned.1.call-done), kind=kOutput, calls=%fused_computation.25 | convolution fusion | flops 3246391296 | bytes 27262976 | tf_op jit(solution)/shard_map/dot_general | solution.py:68
  525.8 4.6 add_convert_fusion
  530.5 30.4 %reduce-scatter.16.cloned.1.call-done = bf16[512,1024]{1,0:T(8,128)(2,1)} async-done(((bf16[1024,1024]{1,0:T(8,128)(2,1)}), bf16[512,1024]{1,0:T(8,128)(2,1)}) %reduce-scatter.16.cloned.1.call-update) | async-done | bytes 1048592 | tf_op jit(solution)/shard_map/reduce_scatter | solution.py:240
  565.6 7.6 convolution_convert_fusion.2
  575.0 6.8 convolution_convert_fusion.1
  583.5 6.8 convolution_convert_fusion
  590.4 8.0 all-gather.32.cloned.1.call-done
  598.4 4.0 convolution_convert_fusion.6
  603.5 6.5 fusion.50
  610.0 5.1 fusion.7
  615.2 5.3 fusion.9
  620.5 4.4 fusion.54
  627.3 11.3 fusion
  638.6 9.5 fusion.43
  649.4 12.5 %fusion.2 = bf16[4,2,512,1024]{2,3,1,0:T(8,128)(2,1)S(1)} fusion(f32[4,1024,512,2]{2,1,3,0:T(8,128)} %get-tuple-element.129, f32[4,2,512,1024]{2,3,1,0:T(8,128)} %get-tuple-element.121, f32[4,2,512]{2,1,0:T(2,128)S(1)} %copy-done.39, f32[4,2,512]{2,1,0:T(2,128)S(1)} %bitcast.246), kind=kLoop, calls=%fused_computation.4 | loop fusion | flops 16777216 | bytes 41975808 | tf_op jit(solution)/shard_map/convert_element_type | solution.py:135
  676.7 3.9 copy.221
  683.5 4.4 multiply_add_fusion
  688.8 4.2 multiply_reduce_fusion
  698.9 4.5 fusion.19
  703.4 5.2 convolution_convert_fusion.3
  716.0 6.0 convolution_convert_fusion.4
  722.1 8.5 convolution_convert_fusion.5
  730.8 7.7 convolution_convert_fusion.7
  742.1 64.2 %reduce-scatter.32.cloned.1.call-done = bf16[96,1024]{1,0:T(8,128)(2,1)} async-done(((bf16[1536,1024]{1,0:T(8,128)(2,1)}), bf16[96,1024]{1,0:T(8,128)(2,1)}) %reduce-scatter.32.cloned.1.call-update) | async-done | bytes 196624 | tf_op jit(solution)/shard_map/reduce_scatter | solution.py:307
  808.1 58.3 %reduce-scatter.22.cloned.1.call-done = bf16[64,512]{1,0:T(8,128)(2,1)} async-done(((bf16[1024,512]{1,0:T(8,128)(2,1)}), bf16[64,512]{1,0:T(8,128)(2,1)}) %reduce-scatter.22.cloned.1.call-update) | async-done | bytes 65552 | tf_op jit(solution)/shard_map/reduce_scatter | solution.py:292
  867.9 58.6 %reduce-scatter.24.cloned.1.call-done = bf16[64,512]{1,0:T(8,128)(2,1)} async-done(((bf16[1024,512]{1,0:T(8,128)(2,1)}), bf16[64,512]{1,0:T(8,128)(2,1)}) %reduce-scatter.24.cloned.1.call-update) | async-done | bytes 65552 | tf_op jit(solution)/shard_map/reduce_scatter | solution.py:295
  928.0 63.1 %reduce-scatter.20.cloned.1.call-done = bf16[64,1024]{1,0:T(8,128)(2,1)} async-done(((bf16[1024,1024]{1,0:T(8,128)(2,1)}), bf16[64,1024]{1,0:T(8,128)(2,1)}) %reduce-scatter.20.cloned.1.call-update) | async-done | bytes 131088 | tf_op jit(solution)/shard_map/reduce_scatter | solution.py:289
  992.8 62.7 %reduce-scatter.26.cloned.1.call-done = bf16[64,1024]{1,0:T(8,128)(2,1)} async-done(((bf16[1024,1024]{1,0:T(8,128)(2,1)}), bf16[64,1024]{1,0:T(8,128)(2,1)}) %reduce-scatter.26.cloned.1.call-update) | async-done | bytes 131088 | tf_op jit(solution)/shard_map/reduce_scatter | solution.py:298
  1057.1 32.1 %reduce-scatter.18.cloned.1.call-done = bf16[512,1024]{1,0:T(8,128)(2,1)} async-done(((bf16[1024,1024]{1,0:T(8,128)(2,1)}), bf16[512,1024]{1,0:T(8,128)(2,1)}) %reduce-scatter.18.cloned.1.call-update) | async-done | bytes 1048592 | tf_op jit(solution)/shard_map/reduce_scatter | solution.py:274
  1091.2 40.0 %all-reduce.2 = (f32[1024]{0:T(1024)}, f32[1024]{0:T(1024)}, f32[128]{0:T(128)}, f32[128]{0:T(128)}) all-reduce(f32[1024]{0:T(1024)S(1)} %get-tuple-element.79, f32[1024]{0:T(1024)S(1)} %copy-done.49, f32[128]{0:T(128)S(1)} %bitcast_reduce_fusion, f32[128]{0:T(128)S(1)} %bitcast_reduce_fusion.1), channel_id=1, replica_groups=mesh['dp'=16,'tensor'=2] {'dp','tensor'}, use_global_device_ids=true, to_apply=%region_19.20 | all-reduce | flops 2304 | bytes 18432 | tf_op jit(solution)/shard_map/psum | solution.py:282
  1131.3 4.2 fusion.30
  (279 shorter events, 131.4 us)
Async XLA Ops:
  7.2 47.2 %all-gather.14.cloned.1.call-start = ((), (), s32[]{:S(2)}) async-start(), calls=%async_computation.12 | async-start | bytes 2228224 | tf_op jit(solution)/shard_map/all_gather | solution.py:176
  7.9 85.2 %all-gather.16.cloned.1.call-start = ((), (), s32[]{:S(2)}) async-start(), calls=%async_computation.13 | async-start | bytes 1114112 | tf_op jit(solution)/shard_map/all_gather | solution.py:177
  8.7 123.5 %all-gather.18.cloned.1.call-start = ((), (), s32[]{:S(2)}) async-start(), calls=%async_computation.14 | async-start | bytes 1114112 | tf_op jit(solution)/shard_map/all_gather | solution.py:178
  9.4 156.8 %all-gather.12.cloned.1.call-start = ((), (), s32[]{:S(2)}) async-start(), calls=%async_computation.11 | async-start | bytes 3145728 | tf_op jit(solution)/shard_map/all_gather | solution.py:189
  14.1 224.3 %all-gather.20.cloned.1.call-start = ((), (), s32[]{:S(2)}) async-start(), calls=%async_computation.15 | async-start | bytes 2228224 | tf_op jit(solution)/shard_map/all_gather | solution.py:179
  14.7 285.3 %reduce-scatter.12.cloned.1.call-start = ((), (), s32[]{:S(2)}) async-start(), calls=%async_computation.16 | async-start | bytes 6291456 | tf_op jit(solution)/shard_map/reduce_scatter | solution.py:208
  17.9 181.0 %copy-start.15 = (f32[1024,64]{1,0:T(8,128)}, f32[1024,64]{1,0:T(8,128)S(1)}, u32[]{:S(2)}) copy-start(f32[1024,64]{1,0:T(8,128)S(1)} %get-tuple-element.118) | copy-start | bytes 786436
  18.0 181.0 %copy-start.17 = (f32[1024,64]{1,0:T(8,128)}, f32[1024,64]{1,0:T(8,128)S(1)}, u32[]{:S(2)}) copy-start(f32[1024,64]{1,0:T(8,128)S(1)} %get-tuple-element.119) | copy-start | bytes 786436
  178.9 19.4 %copy-start.7 = (f32[128,4,8,128]{3,2,1,0:T(8,128)}, f32[128,4,8,128]{3,2,1,0:T(8,128)S(1)}, u32[]{:S(2)}) copy-start(f32[128,4,8,128]{3,2,1,0:T(8,128)S(1)} %get-tuple-element.99) | copy-start | bytes 6291460
  198.3 383.6 %copy-start.37 = (f32[1024,4]{0,1:T(4,128)}, f32[1024,4]{0,1:T(4,128)S(1)}, u32[]{:S(2)}) copy-start(f32[1024,4]{0,1:T(4,128)S(1)} %add_rsqrt_fusion.1) | copy-start | bytes 49156
  199.7 23.6 %copy-start.10 = (bf16[1024,4,64]{2,0,1:T(8,128)(2,1)}, bf16[1024,4,64]{2,0,1:T(8,128)(2,1)S(1)}, u32[]{:S(2)}) copy-start(bf16[1024,4,64]{2,0,1:T(8,128)(2,1)S(1)} %get-tuple-element.112) | copy-start | bytes 1572868
  199.7 23.6 %copy-start.12 = (bf16[1024,4,64]{2,0,1:T(8,128)(2,1)}, bf16[1024,4,64]{2,0,1:T(8,128)(2,1)S(1)}, u32[]{:S(2)}) copy-start(bf16[1024,4,64]{2,0,1:T(8,128)(2,1)S(1)} %get-tuple-element.113) | copy-start | bytes 1572868
  204.0 19.4 %copy-start.19 = (bf16[512,8,128]{2,0,1:T(8,128)(2,1)}, bf16[512,8,128]{2,0,1:T(8,128)(2,1)S(1)}, u32[]{:S(2)}) copy-start(bf16[512,8,128]{2,0,1:T(8,128)(2,1)S(1)} %copy.149) | copy-start | bytes 3145732
  245.2 54.8 %copy-start.5 = (bf16[512,1024]{1,0:T(8,128)(2,1)S(1)}, bf16[512,1024]{1,0:T(8,128)(2,1)}, u32[]{:S(2)}) copy-start(bf16[512,1024]{1,0:T(8,128)(2,1)} %param.26) | copy-start | bytes 3145732
  245.2 56.8 %copy-start.40 = (f32[1024]{0:T(1024)S(1)}, f32[1024]{0:T(1024)}, u32[]{:S(2)}) copy-start(f32[1024]{0:T(1024)} %param.29) | copy-start | bytes 12292
  245.2 102.6 %all-gather.24.cloned.1.call-start = ((), (), s32[]{:S(2)}) async-start(), calls=%async_computation.18 | async-start | bytes 3342336 | tf_op jit(solution)/shard_map/all_gather | solution.py:180
  246.0 135.4 %all-gather.22.cloned.1.call-start = ((), (), s32[]{:S(2)}) async-start(), calls=%async_computation.17 | async-start | bytes 3145728 | tf_op jit(solution)/shard_map/all_gather | solution.py:216
  302.0 261.5 %copy-start.3 = (f32[512,1024]{1,0:T(8,128)}, f32[512,1024]{1,0:T(8,128)S(1)}, u32[]{:S(2)}) copy-start(f32[512,1024]{1,0:T(8,128)S(1)} %get-tuple-element.88) | copy-start | bytes 6291460
  302.0 261.5 %copy-start.42 = (f32[512]{0:T(512)}, f32[512]{0:T(512)S(1)}, u32[]{:S(2)}) copy-start(f32[512]{0:T(512)S(1)} %add_rsqrt_fusion.2) | copy-start | bytes 6148
  303.4 125.8 %all-gather.26.cloned.1.call-start = ((), (), s32[]{:S(2)}) async-start(), calls=%async_computation.19 | async-start | bytes 3342336 | tf_op jit(solution)/shard_map/all_gather | solution.py:181
  304.1 157.9 %all-gather.30.cloned.1.call-start = ((), (), s32[]{:S(2)}) async-start(), calls=%async_computation.22 | async-start | bytes 3145728 | tf_op jit(solution)/shard_map/all_gather | solution.py:230
  304.7 205.1 %all-gather.28.cloned.1.call-start = ((), (), s32[]{:S(2)}) async-start(), calls=%async_computation.20 | async-start | bytes 3342336 | tf_op jit(solution)/shard_map/all_gather | solution.py:182
  305.5 255.4 %reduce-scatter.16.cloned.1.call-start = ((), (), s32[]{:S(2)}) async-start(), calls=%async_computation.23 | async-start | bytes 3145728 | tf_op jit(solution)/shard_map/reduce_scatter | solution.py:240
  509.9 11.8 %copy-start.54 = (bf16[1024,1536]{1,0:T(8,128)(2,1)S(1)}, bf16[1024,1536]{1,0:T(8,128)(2,1)}, u32[]{:S(2)}) copy-start(bf16[1024,1536]{1,0:T(8,128)(2,1)} %all-gather.24.cloned.1.call-done) | copy-start | bytes 9437188
  530.4 33.1 %copy-start.20 = (bf16[512,1024]{1,0:T(8,128)(2,1)S(1)}, bf16[512,1024]{1,0:T(8,128)(2,1)}, u32[]{:S(2)}) copy-start(bf16[512,1024]{1,0:T(8,128)(2,1)} %param.39) | copy-start | bytes 3145732
  530.5 68.0 %all-gather.32.cloned.1.call-start = ((), (), s32[]{:S(2)}) async-start(), calls=%async_computation.24 | async-start | bytes 3145728 | tf_op jit(solution)/shard_map/all_gather | solution.py:251
  565.2 173.4 %reduce-scatter.28.cloned.1.call-start = ((), (), s32[]{:S(2)}) async-start(), calls=%async_computation.30 | async-start | bytes 3342336 | tf_op jit(solution)/shard_map/reduce_scatter | solution.py:301
  573.3 167.1 %reduce-scatter.30.cloned.1.call-start = ((), (), s32[]{:S(2)}) async-start(), calls=%async_computation.31 | async-start | bytes 3342336 | tf_op jit(solution)/shard_map/reduce_scatter | solution.py:304
  581.8 224.6 %reduce-scatter.32.cloned.1.call-start = ((), (), s32[]{:S(2)}) async-start(), calls=%async_computation.32 | async-start | bytes 3342336 | tf_op jit(solution)/shard_map/reduce_scatter | solution.py:307
  590.4 276.0 %reduce-scatter.22.cloned.1.call-start = ((), (), s32[]{:S(2)}) async-start(), calls=%async_computation.27 | async-start | bytes 1114112 | tf_op jit(solution)/shard_map/reduce_scatter | solution.py:292
  615.1 12.1 %slice-start.6 = ((s8[16777216]{0:T(1024)(128)(4,1)}), s8[4194304]{0:T(1024)(128)(4,1)S(1)}, s32[]{:S(2)}) async-start(s8[16777216]{0:T(1024)(128)(4,1)} %bitcast.214), calls=%async_computation.39 | async-start | bytes 8388608
  615.1 12.1 %slice-start.7 = ((s8[16777216]{0:T(1024)(128)(4,1)}), s8[4194304]{0:T(1024)(128)(4,1)S(1)}, s32[]{:S(2)}) async-start(s8[16777216]{0:T(1024)(128)(4,1)} %bitcast.214), calls=%async_computation.40 | async-start | bytes 8388608
  615.1 12.1 %slice-start.8 = ((s8[16777216]{0:T(1024)(128)(4,1)}), s8[4194304]{0:T(1024)(128)(4,1)S(1)}, s32[]{:S(2)}) async-start(s8[16777216]{0:T(1024)(128)(4,1)} %bitcast.214), calls=%async_computation.41 | async-start | bytes 8388608
  638.6 10.8 copy-start.39
  649.3 12.5 %copy-start.14 = (bf16[1024,4,64]{2,0,1:T(8,128)(2,1)S(1)}, bf16[1024,4,64]{2,0,1:T(8,128)(2,1)}, u32[]{:S(2)}) copy-start(bf16[1024,4,64]{2,0,1:T(8,128)(2,1)} %copy-done.12) | copy-start | bytes 1572868
  712.2 214.3 %reduce-scatter.24.cloned.1.call-start = ((), (), s32[]{:S(2)}) async-start(), calls=%async_computation.28 | async-start | bytes 1114112 | tf_op jit(solution)/shard_map/reduce_scatter | solution.py:295
  712.8 278.4 %reduce-scatter.20.cloned.1.call-start = ((), (), s32[]{:S(2)}) async-start(), calls=%async_computation.26 | async-start | bytes 2228224 | tf_op jit(solution)/shard_map/reduce_scatter | solution.py:289
  716.0 339.5 %reduce-scatter.26.cloned.1.call-start = ((), (), s32[]{:S(2)}) async-start(), calls=%async_computation.29 | async-start | bytes 2228224 | tf_op jit(solution)/shard_map/reduce_scatter | solution.py:298
  722.0 367.2 %reduce-scatter.18.cloned.1.call-start = ((), (), s32[]{:S(2)}) async-start(), calls=%async_computation.25 | async-start | bytes 3145728 | tf_op jit(solution)/shard_map/reduce_scatter | solution.py:274
  730.6 400.7 %reduce-scatter.14.cloned.1.call-start = ((), (), s32[]{:S(2)}) async-start(), calls=%async_computation.21 | async-start | bytes 3145728 | tf_op jit(solution)/shard_map/reduce_scatter | solution.py:223
  738.5 350.7 %copy-start.6 = (bf16[512,1024]{1,0:T(8,128)(2,1)S(1)}, bf16[512,1024]{1,0:T(8,128)(2,1)}, u32[]{:S(2)}) copy-start(bf16[512,1024]{1,0:T(8,128)(2,1)} %param.26) | copy-start | bytes 3145732
  738.5 350.7 %copy-start.44 = (f32[1024]{0:T(1024)S(1)}, f32[1024]{0:T(1024)}, u32[]{:S(2)}) copy-start(f32[1024]{0:T(1024)} %param.28) | copy-start | bytes 12292
  738.5 350.7 %copy-start.46 = (f32[512]{0:T(512)S(1)}, f32[512]{0:T(512)}, u32[]{:S(2)}) copy-start(f32[512]{0:T(512)} %copy-done.45) | copy-start | bytes 6148
  738.5 352.8 %copy-start.49 = (f32[1024]{0:T(1024)S(1)}, f32[1024]{0:T(1024)}, u32[]{:S(2)}) copy-start(f32[1024]{0:T(1024)} %get-tuple-element.77) | copy-start | bytes 12292
  738.5 392.8 %copy-start.4 = (f32[512,1024]{1,0:T(8,128)S(1)}, f32[512,1024]{1,0:T(8,128)}, u32[]{:S(2)}) copy-start(f32[512,1024]{1,0:T(8,128)} %copy-done.3) | copy-start | bytes 6291460
  738.5 392.8 %copy-start.41 = (f32[1024]{0:T(1024)S(1)}, f32[1024]{0:T(1024)}, u32[]{:S(2)}) copy-start(f32[1024]{0:T(1024)} %param.29) | copy-start | bytes 12292
  738.5 392.8 %copy-start.43 = (f32[512]{0:T(512)S(1)}, f32[512]{0:T(512)}, u32[]{:S(2)}) copy-start(f32[512]{0:T(512)} %copy-done.42) | copy-start | bytes 6148
  738.5 392.8 %copy-start.48 = (f32[512]{0:T(512)S(1)}, f32[512]{0:T(512)}, u32[]{:S(2)}) copy-start(f32[512]{0:T(512)} %copy-done.47) | copy-start | bytes 6148
  (48 other events, 202.7 us)
Sparse Core Ops, SparseCore 0:
  10.2 44.1 all-gather.13
  56.5 36.5 all-gather.15
  95.3 36.8 all-gather.17
  134.1 32.0 all-gather.11
  168.2 41.4 all-gather.19
  245.3 54.6 reduce-scatter.11
  302.3 45.4 all-gather.23
  349.9 31.4 all-gather.21
  383.7 45.4 all-gather.25
  430.6 31.4 all-gather.29
  464.4 45.4 all-gather.27
  530.6 30.2 reduce-scatter.15
  565.3 33.0 all-gather.31
  602.1 66.3 reduce-scatter.27
  672.1 65.2 reduce-scatter.29
  741.1 65.2 reduce-scatter.31
  809.8 56.5 reduce-scatter.21
  869.9 56.5 reduce-scatter.23
  930.2 60.8 reduce-scatter.19
  994.7 60.6 reduce-scatter.25
  1058.3 30.8 reduce-scatter.17
  1091.4 32.4 reduce-scatter.13
where the time goes:
time: 1150 us; the launch traced here: 1140 us
  waiting for transfers between devices  765 us (67%)
  matrix products  164 us (14%)
  other arithmetic  92.6 us (8%)
  local copies, waits for them, and re-layouts  63.5 us (6%)
  blocking collectives  40 us (3%)
  between operations  15.6 us (1%)
    reduce_scatter x1, waiting for transfers between devices, local(): lax.psum_scatter(grad_down.astype(jnp.bfloat16), 'dp', scatter_dimension=...  64.2 us
    reduce_scatter x1, waiting for transfers between devices, local(): lax.psum_scatter(grad_query_w.astype(jnp.bfloat16), 'dp', scatter_dimensi...  63.1 us
    reduce_scatter x1, waiting for transfers between devices, local(): lax.psum_scatter(grad_out.astype(jnp.bfloat16), 'dp', scatter_dimension=0...  62.7 us
    reduce_scatter x1, waiting for transfers between devices, local(): lax.psum_scatter(grad_value_w.astype(jnp.bfloat16), 'dp', scatter_dimensi...  58.6 us
    reduce_scatter x1, waiting for transfers between devices, local(): lax.psum_scatter(grad_key_w.astype(jnp.bfloat16), 'dp', scatter_dimension...  58.3 us
    reduce_scatter x1, waiting for transfers between devices, local(): lax.psum_scatter(jnp.dot(heads_b, full_out, preferred_element_type=jnp.fl...  53.8 us
    all_gather x1, waiting for transfers between devices, local(): lax.all_gather(down_proj, 'dp', axis=0, tiled=True)  47.8 us
    all_gather x1, waiting for transfers between devices, local(): lax.all_gather(gate_proj, 'dp', axis=0, tiled=True)  42.3 us
  transfers between devices with their start and end apart: 22, of which 18 were waited for; matrix products, arithmetic and copies ran while one was open for 24% of the time, Pallas kernels for 0%

commit v1 on v0

v1 whole, which is shorter than its diff:
```python
import math

import jax
import jax.numpy as jnp
from jax import lax
from jax.sharding import PartitionSpec as P

HD = 128
EPS = 1e-06
THETA = 1000000.0
BF = jnp.bfloat16
F32 = jnp.float32


def rotary_tables(positions, width):
    half_width = width // 2
    freq_index = jnp.arange(half_width).astype(F32)
    inverse_freq = jnp.exp(freq_index * (-2.0 * math.log(THETA) / width))
    angles = positions.astype(F32)[:, None] * inverse_freq[None, :]
    return (jnp.cos(angles)[:, None, :], jnp.sin(angles)[:, None, :])


def rotate(values, cosine_table, sine_table):
    half_width = values.shape[-1] // 2
    lower_half = values[..., :half_width]
    upper_half = values[..., half_width:]
    return jnp.concatenate(
        (
            lower_half * cosine_table - upper_half * sine_table,
            upper_half * cosine_table + lower_half * sine_table,
        ),
        -1,
    )


def rms_unit(values):
    inv_scale = lax.rsqrt(jnp.mean(values * values, -1, keepdims=True) + EPS)
    return (values * inv_scale, inv_scale)


def rms_back(grad_out, gain_vec, unit_vals, inv_scale):
    scaled_grad = grad_out * gain_vec
    return inv_scale * (
        scaled_grad - unit_vals * jnp.mean(scaled_grad * unit_vals, -1, keepdims=True)
    )


def matmul(left, right):
    return jnp.dot(left, right, preferred_element_type=F32)


def contract_rows(left, right):
    return lax.dot_general(left, right, (((0,), (0,)), ((), ())), preferred_element_type=F32)


def contract_cols(left, right):
    return lax.dot_general(left, right, (((1,), (1,)), ((), ())), preferred_element_type=F32)


def attend(query_b, key_b, value_b):
    length = query_b.shape[0]
    block_rows = min(length, 512)
    block_count = length // block_rows
    scale_qk = 1.0 / math.sqrt(query_b.shape[-1])
    outputs = []
    log_sums = []
    for block in range(block_count):
        row_start = block * block_rows
        key_end = row_start + block_rows
        query_block = query_b[row_start:key_end]
        scores = (
            jnp.einsum(
                "qgrd,kgd->grqk", query_block, key_b[:key_end], preferred_element_type=F32
            )
            * scale_qk
        )
        causal = (row_start + jnp.arange(block_rows, dtype=jnp.int32))[:, None] >= jnp.arange(
            key_end, dtype=jnp.int32
        )[None, :]
        scores = jnp.where(causal, scores, -jnp.inf)
        top_score = jnp.max(scores, -1, keepdims=True)
        shifted = jnp.exp(scores - top_score)
        sum_exp = jnp.sum(shifted, -1, keepdims=True)
        probs_b = (shifted / sum_exp).astype(BF)
        outputs.append(
            jnp.einsum("grqk,kgd->qgrd", probs_b, value_b[:key_end], preferred_element_type=F32)
        )
        log_sums.append(top_score + jnp.log(sum_exp))
    return (jnp.concatenate(outputs, 0), log_sums)


def attend_back(query_b, key_b, value_b, grad_b, log_sums):
    length = query_b.shape[0]
    block_rows = min(length, 512)
    block_count = length // block_rows
    scale_qk = 1.0 / math.sqrt(query_b.shape[-1])
    key_acc = jnp.zeros(key_b.shape, F32)
    value_acc = jnp.zeros(key_b.shape, F32)
    grad_queries = []
    for block in range(block_count):
        row_start = block * block_rows
        key_end = row_start + block_rows
        query_block = query_b[row_start:key_end]
        grad_block = grad_b[row_start:key_end]
        keys_seen = key_b[:key_end]
        scores = (
            jnp.einsum("qgrd,kgd->grqk", query_block, keys_seen, preferred_element_type=F32)
            * scale_qk
        )
        causal = (row_start + jnp.arange(block_rows, dtype=jnp.int32))[:, None] >= jnp.arange(
            key_end, dtype=jnp.int32
        )[None, :]
        scores = jnp.where(causal, scores, -jnp.inf)
        probs = jnp.exp(scores - log_sums[block])
        probs_b = probs.astype(BF)
        grad_probs = jnp.einsum(
            "qgrd,kgd->grqk", grad_block, value_b[:key_end], preferred_element_type=F32
        )
        row_dot = jnp.sum(probs * grad_probs, -1, keepdims=True)
        grad_scores_b = (probs * (grad_probs - row_dot)).astype(BF)
        grad_queries.append(
            jnp.einsum("grqk,kgd->qgrd", grad_scores_b, keys_seen, preferred_element_type=F32)
            * scale_qk
        )
        key_acc = key_acc.at[:key_end].add(
            jnp.einsum("grqk,qgrd->kgd", grad_scores_b, query_block, preferred_element_type=F32)
            * scale_qk
        )
        value_acc = value_acc.at[:key_end].add(
            jnp.einsum("grqk,qgrd->kgd", probs_b, grad_block, preferred_element_type=F32)
        )
    return (jnp.concatenate(grad_queries, 0), key_acc, value_acc)


def all_sum(value, sizes):
    for axis, size in sizes:
        if size & (size - 1):
            value = lax.psum(value, axis)
            continue
        step = 1
        while step < size:
            value = value + lax.ppermute(value, axis, [(i, i ^ step) for i in range(size)])
            step *= 2
    return value


def make_local(n_dp, n_tensor):
    paired = n_tensor == 2
    swap = [(0, 1), (1, 0)]

    def gather_rows(own):
        if paired:
            return jnp.concatenate((own, lax.ppermute(own, "tensor", swap)), 0)
        return lax.all_gather(own, "tensor", axis=0, tiled=True)

    def to_sequence(rows):
        if not paired:
            return rows
        half = rows.shape[0] // 2
        first = lax.axis_index("tensor") == 0
        return jnp.concatenate(
            (
                jnp.where(first, rows[:half], rows[half:]),
                jnp.where(first, rows[half:], rows[:half]),
            ),
            0,
        )

    def scatter_rows(part, operand):
        if paired:
            half = operand[0].shape[0] // 2
            sent = part(*(o[half:] for o in operand)).astype(BF)
            got = lax.ppermute(sent, "tensor", swap)
            return part(*(o[:half] for o in operand)) + got.astype(F32)
        return lax.psum_scatter(
            part(*operand).astype(BF), "tensor", scatter_dimension=0, tiled=True
        ).astype(F32)

    def local(
        hidden_in,
        positions,
        gain_attention,
        gain_feedforward,
        gain_query,
        gain_key,
        query_proj,
        key_proj,
        value_proj,
        out_proj,
        gate_proj,
        up_proj,
        down_proj,
        cotangent,
    ):
        length = positions.shape[0]
        own = hidden_in.shape[0]
        width = hidden_in.shape[1]
        heads_here = query_proj.shape[1] // HD
        groups_here = key_proj.shape[1] // HD
        width_query = heads_here * HD
        width_key = groups_here * HD
        width_qkv = width_query + 2 * width_key
        units = gate_proj.shape[1]
        shard_rows = query_proj.shape[0]

        shard_attn = jnp.concatenate(
            (query_proj, key_proj, value_proj, out_proj.reshape(shard_rows, -1)), 1
        )
        shard_mlp = jnp.concatenate((gate_proj, up_proj, down_proj.reshape(shard_rows, -1)), 1)
        full_attn = lax.all_gather(shard_attn, "dp", axis=0, tiled=True)
        full_mlp = lax.all_gather(shard_mlp, "dp", axis=0, tiled=True)
        proj_qkv = full_attn[:, :width_qkv]
        full_out = full_attn[:, width_qkv:].reshape(-1, width)
        full_gateup = full_mlp[:, : 2 * units]
        full_down = full_mlp[:, 2 * units :].reshape(-1, width)

        rows_hidden = gather_rows(hidden_in)
        rows_cot = gather_rows(cotangent)
        cosine_table, sine_table = rotary_tables(positions, HD)
        unit_rows, scale_rows = rms_unit(rows_hidden.astype(F32))
        rows_attn = (unit_rows * gain_attention).astype(BF)
        if paired:
            hidden_f, unit_attn, scale_attn = (
                hidden_in.astype(F32),
                unit_rows[:own],
                scale_rows[:own],
            )
        else:
            hidden_f = hidden_in.astype(F32)
            unit_attn, scale_attn = rms_unit(hidden_f)

        projected = to_sequence(matmul(rows_attn, proj_qkv))
        query_raw = projected[:, :width_query].reshape(length, heads_here, HD)
        key_raw = projected[:, width_query : width_query + width_key].reshape(
            length, groups_here, HD
        )
        value_b = (
            projected[:, width_query + width_key :].astype(BF).reshape(length, groups_here, HD)
        )
        query_unit, query_scale = rms_unit(query_raw)
        key_unit, key_scale = rms_unit(key_raw)
        query_b = (
            rotate(query_unit * gain_query, cosine_table, sine_table)
            .astype(BF)
            .reshape(length, groups_here, heads_here // groups_here, HD)
        )
        key_b = rotate(key_unit * gain_key, cosine_table, sine_table).astype(BF)
        heads_out, log_sums = attend(query_b, key_b, value_b)
        heads_b = to_sequence(heads_out.reshape(length, width_query).astype(BF))
        resid = hidden_f + scatter_rows(lambda h: matmul(h, full_out), (heads_b,))
        unit_mlp, scale_mlp = rms_unit(resid)
        rows_mlp = gather_rows((unit_mlp * gain_feedforward).astype(BF))
        gate_val = matmul(rows_mlp, full_gateup[:, :units])
        up_val = matmul(rows_mlp, full_gateup[:, units:])
        sigmoid_gate = jax.nn.sigmoid(gate_val)
        active_b = (gate_val * sigmoid_gate * up_val).astype(BF)
        output_b = (resid + scatter_rows(lambda a: matmul(a, full_down), (active_b,))).astype(BF)

        grad_active = contract_cols(rows_cot, full_down)
        grad_gate_b = (
            grad_active * up_val * sigmoid_gate * (1.0 + gate_val * (1.0 - sigmoid_gate))
        ).astype(BF)
        grad_up_b = (grad_active * gate_val * sigmoid_gate).astype(BF)
        grad_normed_mlp = scatter_rows(
            lambda g, u: contract_cols(g, full_gateup[:, :units])
            + contract_cols(u, full_gateup[:, units:]),
            (grad_gate_b, grad_up_b),
        )
        grad_mlp_w = jnp.concatenate(
            (
                contract_rows(rows_mlp, grad_gate_b).astype(BF),
                contract_rows(rows_mlp, grad_up_b).astype(BF),
                contract_rows(active_b, rows_cot).astype(BF).reshape(width, -1),
            ),
            1,
        )
        sent_mlp = lax.psum_scatter(grad_mlp_w, "dp", scatter_dimension=0, tiled=True)

        term_feedforward = jnp.sum(grad_normed_mlp * unit_mlp, 0)
        grad_resid = cotangent.astype(F32) + rms_back(
            grad_normed_mlp, gain_feedforward, unit_mlp, scale_mlp
        )
        rows_resid = gather_rows(grad_resid.astype(BF))
        grad_heads_b = (
            to_sequence(contract_cols(rows_resid, full_out).astype(BF))
            .reshape(length, groups_here, heads_here // groups_here, HD)
        )
        grad_qrot, grad_krot, grad_value = attend_back(
            query_b, key_b, value_b, grad_heads_b, log_sums
        )
        grad_qnormed = rotate(
            grad_qrot.reshape(length, heads_here, HD), cosine_table, -sine_table
        )
        grad_knormed = rotate(grad_krot, cosine_table, -sine_table)
        term_query = jnp.sum(grad_qnormed * query_unit, (0, 1))
        term_key = jnp.sum(grad_knormed * key_unit, (0, 1))
        grad_qkv_b = to_sequence(
            jnp.concatenate(
                (
                    rms_back(grad_qnormed, gain_query, query_unit, query_scale).reshape(
                        length, width_query
                    ),
                    rms_back(grad_knormed, gain_key, key_unit, key_scale).reshape(
                        length, width_key
                    ),
                    grad_value.reshape(length, width_key),
                ),
                1,
            ).astype(BF)
        )
        grad_attn_w = jnp.concatenate(
            (
                contract_rows(rows_attn, grad_qkv_b).astype(BF),
                contract_rows(heads_b, rows_resid).astype(BF).reshape(width, -1),
            ),
            1,
        )
        sent_attn = lax.psum_scatter(grad_attn_w, "dp", scatter_dimension=0, tiled=True)
        grad_normed_attn = scatter_rows(lambda g: contract_cols(g, proj_qkv), (grad_qkv_b,))
        term_attention = jnp.sum(grad_normed_attn * unit_attn, 0)
        grad_hidden = grad_resid + rms_back(
            grad_normed_attn, gain_attention, unit_attn, scale_attn
        )
        terms = all_sum(
            jnp.concatenate((term_attention, term_feedforward, term_query, term_key)).reshape(
                -1, HD
            ),
            (("tensor", n_tensor), ("dp", n_dp)),
        ).reshape(-1)
        sent_attn = sent_attn.astype(F32)
        sent_mlp = sent_mlp.astype(F32)
        return (
            output_b,
            grad_hidden,
            terms[:width],
            terms[width : 2 * width],
            terms[2 * width : 2 * width + HD],
            terms[2 * width + HD :],
            sent_attn[:, :width_query],
            sent_attn[:, width_query : width_query + width_key],
            sent_attn[:, width_query + width_key : width_qkv],
            sent_attn[:, width_qkv:].reshape(out_proj.shape),
            sent_mlp[:, :units],
            sent_mlp[:, units : 2 * units],
            sent_mlp[:, 2 * units :].reshape(down_proj.shape),
        )

    return local


def solution(mesh):
    rows = P(("dp", "tensor"), None)
    cut = P("dp", "tensor")
    stacked = P(("tensor", "dp"), None)
    return jax.shard_map(
        make_local(mesh.shape["dp"], mesh.shape["tensor"]),
        mesh=mesh,
        in_specs=(
            rows,
            P("dp"),
            P(),
            P(),
            P(),
            P(),
            cut,
            cut,
            cut,
            stacked,
            cut,
            cut,
            stacked,
            rows,
        ),
        out_specs=(rows, rows, P(), P(), P(), P(), cut, cut, cut, stacked, cut, cut, stacked),
        check_vma=False,
    )
```

time: 1150 us -> 643 us (0.56)
  waiting for transfers between devices: 765 us -> 274 us
  blocking collectives: 40 us -> 0 us
  starting transfers between devices: 1.67 us -> 19.5 us
  matrix products: 164 us -> 152 us
    reduce_scatter x11 -> x2, waiting for transfers between devices: 423 us -> 97.4 us  [the longest x1 97.4 us: local(): lax.psum_scatter(grad_mlp_w, 'dp', scatter_dimension=0, tiled=True)]
    all_gather x11 -> x2, waiting for transfers between devices: 336 us -> 36.1 us  [the longest x1 36.1 us: local(): full_attn = lax.all_gather(shard_attn, 'dp', axis=0, tiled=True)]
    ppermute x0 -> x13, waiting for transfers between devices: none -> 141 us  [the longest x4 64.9 us: scatter_rows(): got = lax.ppermute(sent, 'tensor', swap)]
    psum x1 -> x0, blocking collectives: 40 us -> none  [local(): lax.psum((term_attention, term_feedforward, term_query, term_key), ('dp',...]
    convert_element_type x13 -> x5, other arithmetic: 34.9 us -> 14.2 us  [the longest x2 11.1 us: attend_back(): grad_scores_b = (probs * (grad_probs - row_dot)).astype(BF)]
    ppermute x0 -> x13, starting transfers between devices: none -> 19.3 us  [the longest x5 6.51 us: all_sum(): lax.ppermute(value, axis, [(i, i ^ step) for i in range(size)])]
    reduce_sum x1, other arithmetic: 4.19 us -> 17.1 us  [rms_back(): jnp.mean(scaled_grad * unit_vals, -1, keepdims=True)]
    concatenate x1 -> x6, other arithmetic: 0.26 us -> 12.9 us  [the longest x1 5.26 us: local(): jnp.concatenate((contract_rows(rows_mlp, grad_gate_b).astype(BF), contrac...]
  transfers between devices with their start and end apart: 22 -> 17, of which waited for: 18 -> 13; matrix products, arithmetic and copies ran while one was open for 24% -> 26% of each run, Pallas kernels for 0% -> 0%
where the time goes in v1:
time: 643 us; the launch traced here: 634 us
  waiting for transfers between devices  274 us (43%)
  matrix products  152 us (24%)
  other arithmetic  101 us (16%)
  local copies, waits for them, and re-layouts  70.6 us (11%)
  starting transfers between devices  19.5 us (3%)
  between operations  15.5 us (2%)
    reduce_scatter x1, waiting for transfers between devices, local(): lax.psum_scatter(grad_mlp_w, 'dp', scatter_dimension=0, tiled=True)  97.4 us
    ppermute x4, waiting for transfers between devices, scatter_rows(): got = lax.ppermute(sent, 'tensor', swap)  64.9 us
    ppermute x4, waiting for transfers between devices, gather_rows(): return jnp.concatenate((own, lax.ppermute(own, 'tensor', swap)), 0)  56.4 us
    dot_general x7, matrix products, matmul(): return jnp.dot(left, right, preferred_element_type=F32)  40.6 us
    all_gather x1, waiting for transfers between devices, local(): full_attn = lax.all_gather(shard_attn, 'dp', axis=0, tiled=True)  36.1 us
    dot_general x8, matrix products, contract_cols(): lax.dot_general(left, right, (((1,), (1,)), ((), ())), preferred_element_...  29.2 us
    dot_general x5, matrix products, contract_rows(): lax.dot_general(left, right, (((0,), (0,)), ((), ())), preferred_element_...  28.4 us
    unnamed x213, local copies, waits for them, and re-layouts  23.4 us
  transfers between devices with their start and end apart: 17, of which 13 were waited for; matrix products, arithmetic and copies ran while one was open for 26% of the time, Pallas kernels for 0%

profile of v1, /device:TPU:0, one launch (start us, length us, event | category | flops | bytes accessed | tf_op | source)
XLA Modules:
  0.0 633.6 jit_solution(4155793221985874017)
XLA Ops:
  12.2 3.1 collective-permute-start
  17.3 2.9 fusion.117
  20.3 18.2 %collective-permute-done = bf16[512,1024]{1,0:T(8,128)(2,1)S(1)} collective-permute-done((bf16[512,1024]{1,0:T(8,128)(2,1)S(1)}, bf16[512,1024]{1,0:T(8,128)(2,1)S(1)}, u32[]{:S(2)}, u32[]{:S(2)}) %collective-permute-start) | collective-permute-done | bytes 1048608 | tf_op jit(solution)/shard_map/ppermute | solution.py:153
  39.0 36.1 %all-gather.3.cloned.1.call-done = bf16[1024,3072]{1,0:T(8,128)(2,1)} async-done(((bf16[64,3072]{1,0:T(8,128)(2,1)}), bf16[1024,3072]{1,0:T(8,128)(2,1)}) %all-gather.3.cloned.1.call-update) | async-done | bytes 6291472 | tf_op jit(solution)/shard_map/all_gather | solution.py:210
  75.0 10.0 %fusion.36 = f32[1024,2048]{1,0:T(8,128)} fusion(bf16[1024,3072]{1,0:T(8,128)(2,1)} %all-gather.3.cloned.1.call-done, f32[1024]{0:T(1024)S(1)} %copy-done.74, f32[1024]{0:T(1024)S(1)} %add_rsqrt_fusion.2, bf16[512,1024]{1,0:T(8,128)(2,1)S(1)} %collective-permute-done, bf16[512,1024]{1,0:T(8,128)(2,1)S(1)} %copy-done.40), kind=kOutput, calls=%fused_computation.77 | convolution fusion | flops 4302307328 | bytes 14688256 | tf_op jit(solution)/shard_map/dot_general | solution.py:49
  85.0 4.3 slice_select_fusion.1
  89.4 3.3 fusion.5
  107.3 3.7 multiply_reduce_fusion.8
  125.7 7.5 %fusion.135 = (f32[4,2,512]{2,1,0:T(2,128)S(1)}, f32[4,2,512,1024]{2,3,1,0:T(8,128)}) fusion(bf16[512,4,2,128]{3,0,2,1:T(8,128)(2,1)S(1)} %bitcast.234, bf16[1024,4,64]{2,0,1:T(8,128)(2,1)S(1)} %get-tuple-element.107, bf16[1024,4,64]{2,0,1:T(8,128)(2,1)S(1)} %get-tuple-element.106, pred[512,1024]{0,1:T(8,128)(4,1)S(1)} %copy-done.58), kind=kOutput, calls=%fused_computation.226 | convolution fusion | flops 1088417792 | bytes 19415040 | tf_op jit(solution)/shard_map/qgrd,kgd->grqk/dot_general | solution.py:72
  133.2 8.3 %fusion.3 = f32[4,2,512]{2,1,0:T(2,128)S(1)} fusion(f32[4,2,512,1024]{2,3,1,0:T(8,128)} %get-tuple-element.129, f32[4,2,512]{2,1,0:T(2,128)S(1)} %get-tuple-element.128), kind=kLoop, calls=%fused_computation.9 | loop fusion | flops 8384512 | bytes 16809984 | tf_op jit(solution)/shard_map/reduce_sum | solution.py:83
  141.6 7.8 %fusion.80 = bf16[4,128,2,512]{3,1,2,0:T(8,128)(2,1)S(1)} fusion(f32[4,2,512,1024]{2,3,1,0:T(8,128)} %get-tuple-element.129, f32[4,2,512]{2,1,0:T(2,128)S(1)} %fusion.3, f32[4,2,512]{2,1,0:T(2,128)S(1)} %get-tuple-element.128, bf16[1024,4,128,1]{2,1,0,3:T(4,128)(2,1)S(1)} %bitcast.237), kind=kOutput, calls=%fused_computation.156 | convolution fusion | flops 1086849024 | bytes 18907136 | tf_op jit(solution)/shard_map/grqk,kgd->qgrd/dot_general | solution.py:86
  151.8 3.6 fusion.84
  157.6 24.0 %collective-permute-done.1 = bf16[512,1024]{1,0:T(8,128)(2,1)S(1)} collective-permute-done((bf16[512,1024]{1,0:T(8,128)(2,1)S(1)}, bf16[512,1024]{1,0:T(8,128)(2,1)S(1)}, u32[]{:S(2)}, u32[]{:S(2)}) %collective-permute-start.1) | collective-permute-done | bytes 1048608 | tf_op jit(solution)/shard_map/ppermute | solution.py:173
  181.6 3.2 multiply_reduce_fusion.7
  188.9 15.2 %collective-permute-done.4 = bf16[512,1024]{1,0:T(8,128)(2,1)S(1)} collective-permute-done((bf16[512,1024]{1,0:T(8,128)(2,1)S(1)}, bf16[512,1024]{1,0:T(8,128)(2,1)S(1)}, u32[]{:S(2)}, u32[]{:S(2)}) %collective-permute-start.4) | collective-permute-done | bytes 1048608 | tf_op jit(solution)/shard_map/ppermute | solution.py:153
  205.1 3.7 slice.345
  208.8 5.9 reshape.389
  214.7 8.8 %fusion.136 = f32[1024,1536]{1,0:T(8,128)} fusion(bf16[1024,1024]{1,0:T(8,128)(2,1)} %constant_dynamic-update-slice_fusion, bf16[1536,1024]{1,0:T(8,128)(2,1)} %reshape.389), kind=kOutput, calls=%fused_computation.227 | convolution fusion | flops 3221225472 | bytes 11534336 | tf_op jit(solution)/shard_map/dot_general | solution.py:57
  225.9 8.6 %fusion.42 = f32[1024,1536]{1,0:T(8,128)} fusion(bf16[1024,4608]{1,0:T(8,128)(2,1)} %all-gather.5.cloned.1.call-done, bf16[512,1024]{1,0:T(8,128)(2,1)} %collective-permute-done.2, bf16[512,1024]{1,0:T(8,128)(2,1)} %multiply_convert_fusion.4), kind=kOutput, calls=%fused_computation.83 | convolution fusion | flops 3225419776 | bytes 11534336 | tf_op jit(solution)/shard_map/dot_general | solution.py:49
  234.5 10.6 %multiply_convert_fusion.1 = (bf16[1024,1536]{1,0:T(8,128)(2,1)S(1)}, bf16[1024,1536]{1,0:T(8,128)(2,1)}, bf16[1024,1536]{1,0:T(8,128)(2,1)S(1)}) fusion(f32[1024,1536]{1,0:T(8,128)} %fusion.136, f32[1024,1536]{1,0:T(8,128)} %fusion.42, bf16[1024,4608]{1,0:T(8,128)(2,1)S(1)} %bitcast.242, bf16[512,1024]{1,0:T(8,128)(2,1)} %collective-permute-done.2, ...), kind=kOutput, calls=%fused_computation.34 | convolution fusion | flops 3250585600 | bytes 27262976 | tf_op jit(solution)/shard_map/dot_general | solution.py:49
  252.2 21.1 %collective-permute-done.5 = bf16[512,1024]{1,0:T(8,128)(2,1)S(1)} collective-permute-done((bf16[512,1024]{1,0:T(8,128)(2,1)S(1)}, bf16[512,1024]{1,0:T(8,128)(2,1)S(1)}, u32[]{:S(2)}, u32[]{:S(2)}) %collective-permute-start.5) | collective-permute-done | bytes 1048608 | tf_op jit(solution)/shard_map/ppermute | solution.py:173
  273.3 2.8 multiply_reduce_fusion.2
  281.0 20.6 %collective-permute-done.6 = bf16[512,1024]{1,0:T(8,128)(2,1)S(1)} collective-permute-done((bf16[512,1024]{1,0:T(8,128)(2,1)}, bf16[512,1024]{1,0:T(8,128)(2,1)S(1)}, u32[]{:S(2)}, u32[]{:S(2)}) %collective-permute-start.6) | collective-permute-done | bytes 1048608 | tf_op jit(solution)/shard_map/ppermute | solution.py:153
  301.6 4.7 convolution_convert_fusion.3
  309.4 2.7 fusion.10
  319.2 11.2 %fusion = (f32[4,2,512]{2,1,0:T(2,128)}, f32[4,1024,512,2]{2,1,3,0:T(8,128)}) fusion(f32[4,2,512,1024]{2,3,1,0:T(8,128)S(1)} %bitcast.217, f32[4,2,512]{2,1,0:T(2,128)} %bitcast.246, bf16[512,4,2,128]{0,3,2,1:T(8,128)(2,1)} %bitcast.230, bf16[1024,4,128,1]{2,1,0,3:T(4,128)(2,1)} %bitcast.236), kind=kOutput, calls=%fused_computation.2 | convolution fusion | flops 1086320640 | bytes 35684352 | tf_op jit(solution)/shard_map/qgrd,kgd->grqk/dot_general | solution.py:116
  330.5 8.4 %fusion.2 = bf16[4,2,512,1024]{2,3,1,0:T(8,128)(2,1)S(1)} fusion(f32[4,1024,512,2]{2,1,3,0:T(8,128)} %get-tuple-element.136, f32[4,2,512,1024]{2,3,1,0:T(8,128)S(1)} %bitcast.217, f32[4,2,512]{2,1,0:T(2,128)} %get-tuple-element.135, f32[4,2,512]{2,1,0:T(2,128)} %bitcast.247), kind=kLoop, calls=%fused_computation.4 | loop fusion | flops 16777216 | bytes 41975808 | tf_op jit(solution)/shard_map/convert_element_type | solution.py:120
  344.5 3.9 copy.226
  348.4 2.7 copy.227
  351.2 4.1 multiply_subtract_fusion
  356.0 17.1 %multiply_reduce_fusion = (f32[1024,8]{1,0:T(8,128)S(1)}, f32[1024,8,128]{2,1,0:T(8,128)}) fusion(f32[1024,8,128]{2,1,0:T(8,128)S(1)} %bitcast.221, f32[128]{0:T(128)S(1)} %copy-done.71, f32[1024,8]{1,0:T(8,128)S(1)} %copy-done.27, f32[1024,8,64]{2,1,0:T(8,128)S(1)} %get-tuple-element.89, f32[1024,8,64]{2,1,0:T(8,128)S(1)} %get-tuple-element.88), kind=kLoop, calls=%fused_computation.57 | loop fusion | flops 5234688 | bytes 12648960 | tf_op jit(solution)/shard_map/reduce_sum | solution.py:44
  377.8 2.8 fusion.111
  381.7 9.9 %fusion.59 = bf16[1024,4,128]{0,2,1:T(8,128)(2,1)} fusion(f32[512,4,128]{0,2,1:T(8,128)} %fusion.100, bf16[512,4,2,128]{0,3,2,1:T(8,128)(2,1)S(1)} %bitcast.231, f32[4,2,512,1024]{2,3,1,0:T(8,128)} %get-tuple-element.129, f32[4,2,512]{2,1,0:T(2,128)S(1)} %bitcast.248), kind=kOutput, calls=%fused_computation.112 | convolution fusion | flops 1083179008 | bytes 19939328 | tf_op jit(solution)/shard_map/grqk,qgrd->kgd/dot_general | solution.py:130
  398.5 7.0 %fusion.22 = (f32[1024]{0:T(1024)S(1)}, bf16[1024,1024]{1,0:T(8,128)(2,1)S(1)}) fusion(f32[128,8,8,128]{3,2,1,0:T(8,128)} %bitcast.222, f32[128,8,8,128]{3,2,1,0:T(8,128)S(1)} %bitcast.225, f32[512,2048]{1,0:T(8,128)S(1)} %copy-done.4, f32[512,2048]{1,0:T(8,128)S(1)} %copy-done.2, f32[128,8,8,128]{3,2,1,0:T(8,128)S(1)} %bitcast.224, ...), kind=kLoop, calls=%fused_computation.48 | loop fusion | flops 11533312 | bytes 23076864 | tf_op jit(solution)/shard_map/reduce_sum | solution.py:295
  411.7 4.5 fusion.60
  416.3 5.3 fusion.29
  421.5 3.2 pad_maximum_fusion.2
  426.6 6.7 %convolution_convert_fusion = bf16[1536,1024]{1,0:T(8,128)(2,1)} fusion(bf16[1024,1536]{1,0:T(8,128)(2,1)S(1)} %copy-done.84, bf16[1024,1024]{1,0:T(8,128)(2,1)} %constant_dynamic-update-slice_fusion), kind=kOutput, calls=%fused_computation.70 | convolution fusion | flops 3222798336 | bytes 8388608 | tf_op jit(solution)/shard_map/dot_general | solution.py:53
  433.3 4.6 reshape.393
  437.9 6.5 %convolution_convert_fusion.2 = bf16[1024,1536]{1,0:T(8,128)(2,1)S(1)} fusion(bf16[1024,1536]{1,0:T(8,128)(2,1)} %copy-done.83, bf16[512,1024]{1,0:T(8,128)(2,1)} %collective-permute-done.2, bf16[512,1024]{1,0:T(8,128)(2,1)} %multiply_convert_fusion.4), kind=kOutput, calls=%fused_computation.72 | convolution fusion | flops 3226992640 | bytes 8388608 | tf_op jit(solution)/shard_map/dot_general | solution.py:53
  444.4 5.4 convolution_convert_fusion.1
  449.9 5.3 pad_maximum_fusion.1
  456.8 4.7 fusion.87
  467.8 19.8 %collective-permute-done.7 = bf16[512,1024]{1,0:T(8,128)(2,1)S(1)} collective-permute-done((bf16[512,1024]{1,0:T(8,128)(2,1)S(1)}, bf16[512,1024]{1,0:T(8,128)(2,1)S(1)}, u32[]{:S(2)}, u32[]{:S(2)}) %collective-permute-start.7) | collective-permute-done | bytes 1048608 | tf_op jit(solution)/shard_map/ppermute | solution.py:173
  487.6 2.7 multiply_reduce_fusion.3
  491.9 15.5 %collective-permute-done.8 = f32[18,128]{1,0:T(8,128)S(1)} collective-permute-done((f32[18,128]{1,0:T(8,128)S(1)}, f32[18,128]{1,0:T(8,128)S(1)}, u32[]{:S(2)}, u32[]{:S(2)}) %collective-permute-start.8) | collective-permute-done | bytes 9248 | tf_op jit(solution)/shard_map/ppermute | solution.py:142
  510.6 2.8 add_convert_fusion.2
  526.2 97.4 %reduce-scatter.5.cloned.1.call-done = bf16[64,4608]{1,0:T(8,128)(2,1)} async-done(((bf16[1024,4608]{1,0:T(8,128)(2,1)}), bf16[64,4608]{1,0:T(8,128)(2,1)}) %reduce-scatter.5.cloned.1.call-update) | async-done | bytes 589840 | tf_op jit(solution)/shard_map/reduce_scatter | solution.py:277
  (330 shorter events, 125.8 us)
Async XLA Ops:
  7.2 67.8 %all-gather.3.cloned.1.call-start = ((), (), s32[]{:S(2)}) async-start(), calls=%async_computation.2 | async-start | bytes 6684672 | tf_op jit(solution)/shard_map/all_gather | solution.py:210
  9.2 195.9 %all-gather.5.cloned.1.call-start = ((), (), s32[]{:S(2)}) async-start(), calls=%async_computation.3 | async-start | bytes 10027008 | tf_op jit(solution)/shard_map/all_gather | solution.py:211
  10.3 64.8 %copy-start.74 = (f32[1024]{0:T(1024)S(1)}, f32[1024]{0:T(1024)}, u32[]{:S(2)}) copy-start(f32[1024]{0:T(1024)} %param.28) | copy-start | bytes 12292
  12.2 510.6 %reduce-scatter.3.cloned.1.call-start = ((), (), s32[]{:S(2)}) async-start(), calls=%async_computation.4 | async-start | bytes 6684672 | tf_op jit(solution)/shard_map/reduce_scatter | solution.py:318
  12.2 26.2 %collective-permute-start = (bf16[512,1024]{1,0:T(8,128)(2,1)S(1)}, bf16[512,1024]{1,0:T(8,128)(2,1)S(1)}, u32[]{:S(2)}, u32[]{:S(2)}) collective-permute-start(bf16[512,1024]{1,0:T(8,128)(2,1)S(1)} %copy-done.40), channel_id=1, source_target_pairs={{0,1},{1,0},{2,3},{3,2},{4,5},{5,4},{6,7},{7,6},{8,9},{9,8},{10,11... | collective-permute-start | bytes 3145736 | tf_op jit(solution)/shard_map/ppermute | solution.py:153
  20.3 79.7 %copy-start.15 = (f32[1024,64]{1,0:T(8,128)}, f32[1024,64]{1,0:T(8,128)S(1)}, u32[]{:S(2)}) copy-start(f32[1024,64]{1,0:T(8,128)S(1)} %get-tuple-element.125) | copy-start | bytes 786436
  20.3 79.7 %copy-start.34 = (f32[1024,64]{1,0:T(8,128)}, f32[1024,64]{1,0:T(8,128)S(1)}, u32[]{:S(2)}) copy-start(f32[1024,64]{1,0:T(8,128)S(1)} %get-tuple-element.124) | copy-start | bytes 786436
  38.5 46.6 %copy-start.44 = (bf16[512,1024]{1,0:T(8,128)(2,1)}, bf16[512,1024]{1,0:T(8,128)(2,1)S(1)}, u32[]{:S(2)}) copy-start(bf16[512,1024]{1,0:T(8,128)(2,1)S(1)} %collective-permute-done) | copy-start | bytes 3145732
  39.0 46.1 %copy-start.67 = (f32[1024]{0:T(1024)}, f32[1024]{0:T(1024)S(1)}, u32[]{:S(2)}) copy-start(f32[1024]{0:T(1024)S(1)} %add_rsqrt_fusion.2) | copy-start | bytes 12292
  89.4 15.4 %copy-start.1 = (f32[512,2048]{1,0:T(8,128)}, f32[512,2048]{1,0:T(8,128)S(1)}, u32[]{:S(2)}) copy-start(f32[512,2048]{1,0:T(8,128)S(1)} %get-tuple-element.90) | copy-start | bytes 12582916
  89.4 15.4 %copy-start.3 = (f32[512,2048]{1,0:T(8,128)}, f32[512,2048]{1,0:T(8,128)S(1)}, u32[]{:S(2)}) copy-start(f32[512,2048]{1,0:T(8,128)S(1)} %get-tuple-element.91) | copy-start | bytes 12582916
  105.1 12.8 %copy-start.8 = (f32[1024,512]{1,0:T(8,128)}, f32[1024,512]{1,0:T(8,128)S(1)}, u32[]{:S(2)}) copy-start(f32[1024,512]{1,0:T(8,128)S(1)} %fusion.50) | copy-start | bytes 6291460
  117.9 161.4 %copy-start.60 = (f32[1024,4]{0,1:T(4,128)}, f32[1024,4]{0,1:T(4,128)S(1)}, u32[]{:S(2)}) copy-start(f32[1024,4]{0,1:T(4,128)S(1)} %add_rsqrt_fusion.1) | copy-start | bytes 49156
  133.2 16.2 %slice-start = ((s8[8388608]{0:T(1024)(128)(4,1)}), s8[4194304]{0:T(1024)(128)(4,1)S(1)}, s32[]{:S(2)}) async-start(s8[8388608]{0:T(1024)(128)(4,1)} %bitcast.212), calls=%async_computation.6 | async-start | bytes 8388608
  151.8 29.8 %copy-start.79 = (bf16[4,128,2,512]{3,1,2,0:T(8,128)(2,1)}, bf16[4,128,2,512]{3,1,2,0:T(8,128)(2,1)S(1)}, u32[]{:S(2)}) copy-start(bf16[4,128,2,512]{3,1,2,0:T(8,128)(2,1)S(1)} %get-tuple-element.110) | copy-start | bytes 3145732
  151.8 29.8 %copy-start.41 = (bf16[512,1024]{1,0:T(8,128)(2,1)S(1)}, bf16[512,1024]{1,0:T(8,128)(2,1)}, u32[]{:S(2)}) copy-start(bf16[512,1024]{1,0:T(8,128)(2,1)} %param.26) | copy-start | bytes 3145732
  155.5 26.1 %collective-permute-start.1 = (bf16[512,1024]{1,0:T(8,128)(2,1)S(1)}, bf16[512,1024]{1,0:T(8,128)(2,1)S(1)}, u32[]{:S(2)}, u32[]{:S(2)}) collective-permute-start(bf16[512,1024]{1,0:T(8,128)(2,1)S(1)} %fusion.84), channel_id=1, source_target_pairs={{0,1},{1,0},{2,3},{3,2},{4,5},{5,4},{6,7},{7,6},{8,9},{9,8},{10,11... | collective-permute-start | bytes 3145736 | tf_op jit(solution)/shard_map/ppermute | solution.py:173
  157.1 46.9 %collective-permute-start.4 = (bf16[512,1024]{1,0:T(8,128)(2,1)S(1)}, bf16[512,1024]{1,0:T(8,128)(2,1)S(1)}, u32[]{:S(2)}, u32[]{:S(2)}) collective-permute-start(bf16[512,1024]{1,0:T(8,128)(2,1)S(1)} %copy-done.23), channel_id=1, source_target_pairs={{0,1},{1,0},{2,3},{3,2},{4,5},{5,4},{6,7},{7,6},{8,9},{9,8},{10,11... | collective-permute-start | bytes 3145736 | tf_op jit(solution)/shard_map/ppermute | solution.py:153
  184.7 91.4 %copy-start.10 = (f32[512,1024]{1,0:T(8,128)}, f32[512,1024]{1,0:T(8,128)S(1)}, u32[]{:S(2)}) copy-start(f32[512,1024]{1,0:T(8,128)S(1)} %get-tuple-element.131) | copy-start | bytes 6291460
  184.7 91.4 %copy-start.65 = (f32[512]{0:T(512)}, f32[512]{0:T(512)S(1)}, u32[]{:S(2)}) copy-start(f32[512]{0:T(512)S(1)} %add_rsqrt_fusion.3) | copy-start | bytes 6148
  186.3 39.6 %collective-permute-start.2 = (bf16[512,1024]{1,0:T(8,128)(2,1)}, bf16[512,1024]{1,0:T(8,128)(2,1)}, u32[]{:S(2)}, u32[]{:S(2)}) collective-permute-start(bf16[512,1024]{1,0:T(8,128)(2,1)} %multiply_convert_fusion.4), channel_id=1, source_target_pairs={{0,1},{1,0},{2,3},{3,2},{4,5},{5,4},{6,7},{7,6},{8,9},{9,8},{10,11... | collective-permute-start | bytes 3145736 | tf_op jit(solution)/shard_map/ppermute | solution.py:153
  214.7 19.8 %slice-start.11 = ((s8[9437184]{0:T(1024)(128)(4,1)}), s8[4194304]{0:T(1024)(128)(4,1)S(1)}, s32[]{:S(2)}) async-start(s8[9437184]{0:T(1024)(128)(4,1)} %bitcast.241), calls=%async_computation.17 | async-start | bytes 8388608
  214.7 19.8 %slice-start.12 = ((s8[9437184]{0:T(1024)(128)(4,1)}), s8[4194304]{0:T(1024)(128)(4,1)S(1)}, s32[]{:S(2)}) async-start(s8[9437184]{0:T(1024)(128)(4,1)} %bitcast.241), calls=%async_computation.18 | async-start | bytes 8388608
  223.5 11.0 %slice-start.13 = ((s8[9437184]{0:T(1024)(128)(4,1)}), s8[1048576]{0:T(1024)(128)(4,1)S(1)}, s32[]{:S(2)}) async-start(s8[9437184]{0:T(1024)(128)(4,1)} %bitcast.241), calls=%async_computation.19 | async-start | bytes 2097152
  245.1 28.2 %copy-start.83 = (bf16[1024,1536]{1,0:T(8,128)(2,1)}, bf16[1024,1536]{1,0:T(8,128)(2,1)S(1)}, u32[]{:S(2)}) copy-start(bf16[1024,1536]{1,0:T(8,128)(2,1)S(1)} %get-tuple-element.85) | copy-start | bytes 9437188
  248.8 24.5 %collective-permute-start.5 = (bf16[512,1024]{1,0:T(8,128)(2,1)S(1)}, bf16[512,1024]{1,0:T(8,128)(2,1)S(1)}, u32[]{:S(2)}, u32[]{:S(2)}) collective-permute-start(bf16[512,1024]{1,0:T(8,128)(2,1)S(1)} %add_convert_fusion.1), channel_id=1, source_target_pairs={{0,1},{1,0},{2,3},{3,2},{4,5},{5,4},{6,7},{7,6},{8,9},{9,8},{10,11... | collective-permute-start | bytes 3145736 | tf_op jit(solution)/shard_map/ppermute | solution.py:173
  252.2 24.0 %copy-start.24 = (bf16[512,1024]{1,0:T(8,128)(2,1)S(1)}, bf16[512,1024]{1,0:T(8,128)(2,1)}, u32[]{:S(2)}) copy-start(bf16[512,1024]{1,0:T(8,128)(2,1)} %param.39) | copy-start | bytes 3145732
  277.8 23.8 %collective-permute-start.6 = (bf16[512,1024]{1,0:T(8,128)(2,1)}, bf16[512,1024]{1,0:T(8,128)(2,1)S(1)}, u32[]{:S(2)}, u32[]{:S(2)}) collective-permute-start(bf16[512,1024]{1,0:T(8,128)(2,1)} %fusion.128), channel_id=1, source_target_pairs={{0,1},{1,0},{2,3},{3,2},{4,5},{5,4},{6,7},{7,6},{8,9},{9,8},{10,11... | collective-permute-start | bytes 3145736 | tf_op jit(solution)/shard_map/ppermute | solution.py:153
  280.3 27.1 %slice-start.2 = ((s8[8388608]{0:T(1024)(128)(4,1)}), s8[4194304]{0:T(1024)(128)(4,1)S(1)}, s32[]{:S(2)}) async-start(s8[8388608]{0:T(1024)(128)(4,1)} %bitcast.214), calls=%async_computation.8 | async-start | bytes 8388608
  281.0 26.5 %slice-start.3 = ((s8[8388608]{0:T(1024)(128)(4,1)}), s8[4194304]{0:T(1024)(128)(4,1)S(1)}, s32[]{:S(2)}) async-start(s8[8388608]{0:T(1024)(128)(4,1)} %bitcast.214), calls=%async_computation.9 | async-start | bytes 8388608
  351.2 22.7 %slice-start.8 = ((s8[8388608]{0:T(1024)(128)(4,1)}), s8[4194304]{0:T(1024)(128)(4,1)S(1)}, s32[]{:S(2)}) async-start(s8[8388608]{0:T(1024)(128)(4,1)} %bitcast.218), calls=%async_computation.14 | async-start | bytes 8388608
  355.9 17.9 %slice-start.9 = ((s8[8388608]{0:T(1024)(128)(4,1)}), s8[4194304]{0:T(1024)(128)(4,1)S(1)}, s32[]{:S(2)}) async-start(s8[8388608]{0:T(1024)(128)(4,1)} %bitcast.218), calls=%async_computation.15 | async-start | bytes 8388608
  355.9 17.9 %copy-start.37 = (bf16[512,8,128]{2,0,1:T(8,128)(2,1)S(1)}, bf16[512,8,128]{2,0,1:T(8,128)(2,1)}, u32[]{:S(2)}) copy-start(bf16[512,8,128]{2,0,1:T(8,128)(2,1)} %copy.156) | copy-start | bytes 3145732
  356.0 17.9 %copy-start.39 = (f32[512,4,128]{2,0,1:T(8,128)S(1)}, f32[512,4,128]{2,0,1:T(8,128)}, u32[]{:S(2)}) copy-start(f32[512,4,128]{2,0,1:T(8,128)} %fusion.104) | copy-start | bytes 3145732
  424.7 198.9 %reduce-scatter.5.cloned.1.call-start = ((), (), s32[]{:S(2)}) async-start(), calls=%async_computation.5 | async-start | bytes 10027008 | tf_op jit(solution)/shard_map/reduce_scatter | solution.py:277
  461.5 26.1 %collective-permute-start.7 = (bf16[512,1024]{1,0:T(8,128)(2,1)S(1)}, bf16[512,1024]{1,0:T(8,128)(2,1)S(1)}, u32[]{:S(2)}, u32[]{:S(2)}) collective-permute-start(bf16[512,1024]{1,0:T(8,128)(2,1)S(1)} %fusion.87), channel_id=1, source_target_pairs={{0,1},{1,0},{2,3},{3,2},{4,5},{5,4},{6,7},{7,6},{8,9},{9,8},{10,11... | collective-permute-start | bytes 3145736 | tf_op jit(solution)/shard_map/ppermute | solution.py:173
  463.0 24.5 %slice-start.15 = ((s8[6291456]{0:T(1024)(128)(4,1)}), s8[4194304]{0:T(1024)(128)(4,1)S(1)}, s32[]{:S(2)}) async-start(s8[6291456]{0:T(1024)(128)(4,1)} %bitcast.253), calls=%async_computation.21 | async-start | bytes 8388608
  464.3 23.2 %copy-start.55 = (bf16[512,2048]{1,0:T(8,128)(2,1)S(1)}, bf16[512,2048]{1,0:T(8,128)(2,1)}, u32[]{:S(2)}) copy-start(bf16[512,2048]{1,0:T(8,128)(2,1)} %copy-done.54) | copy-start | bytes 6291460
  464.3 23.2 %slice-start.16 = ((s8[6291456]{0:T(1024)(128)(4,1)}), s8[2097152]{0:T(1024)(128)(4,1)S(1)}, s32[]{:S(2)}) async-start(s8[6291456]{0:T(1024)(128)(4,1)} %bitcast.253), calls=%async_computation.22 | async-start | bytes 4194304
  466.1 44.4 %collective-permute-start.3 = (bf16[512,1024]{1,0:T(8,128)(2,1)S(1)}, bf16[512,1024]{1,0:T(8,128)(2,1)S(1)}, u32[]{:S(2)}, u32[]{:S(2)}) collective-permute-start(bf16[512,1024]{1,0:T(8,128)(2,1)S(1)} %fusion.81), channel_id=1, source_target_pairs={{0,1},{1,0},{2,3},{3,2},{4,5},{5,4},{6,7},{7,6},{8,9},{9,8},{10,11... | collective-permute-start | bytes 3145736 | tf_op jit(solution)/shard_map/ppermute | solution.py:173
  467.7 22.6 %copy-start.64 = (f32[1024]{0:T(1024)S(1)}, f32[1024]{0:T(1024)}, u32[]{:S(2)}) copy-start(f32[1024]{0:T(1024)} %get-tuple-element.79) | copy-start | bytes 12292
  467.7 42.8 %copy-start.11 = (f32[512,1024]{1,0:T(8,128)S(1)}, f32[512,1024]{1,0:T(8,128)}, u32[]{:S(2)}) copy-start(f32[512,1024]{1,0:T(8,128)} %copy-done.10) | copy-start | bytes 6291460
  490.3 17.1 %collective-permute-start.8 = (f32[18,128]{1,0:T(8,128)S(1)}, f32[18,128]{1,0:T(8,128)S(1)}, u32[]{:S(2)}, u32[]{:S(2)}) collective-permute-start(f32[18,128]{1,0:T(8,128)S(1)} %maximum_bitcast_fusion.3), channel_id=1, source_target_pairs={{0,1},{1,0},{2,3},{3,2},{4,5},{5,4},{6,7},{7,6},{8,9},{9,8},{10,11... | collective-permute-start | bytes 27656 | tf_op jit(solution)/shard_map/ppermute | solution.py:142
  507.5 1.2 collective-permute-start.9
  508.6 10.1 %copy-start.25 = (bf16[512,1024]{1,0:T(8,128)(2,1)S(1)}, bf16[512,1024]{1,0:T(8,128)(2,1)}, u32[]{:S(2)}) copy-start(bf16[512,1024]{1,0:T(8,128)(2,1)} %param.39) | copy-start | bytes 3145732
  508.7 4.6 collective-permute-start.10
  513.3 3.7 collective-permute-start.11
  517.0 4.6 collective-permute-start.12
  (75 other events, 327.3 us)
Sparse Core Ops, SparseCore 0:
  10.9 64.1 all-gather.2
  77.3 79.5 all-gather.4
  424.8 84.4 reduce-scatter.2
  513.3 110.3 reduce-scatter.4

commit v2 on v1

v2 whole, which is shorter than its diff:
```python
import functools
import math

import jax
import jax.numpy as jnp
from jax import lax
from jax.experimental import pallas as pl
from jax.experimental.pallas import tpu as pltpu
from jax.sharding import PartitionSpec as P

HD = 128
EPS = 1e-06
THETA = 1000000.0
BF = jnp.bfloat16
F32 = jnp.float32


def rotary_tables(positions, width):
    half_width = width // 2
    freq_index = jnp.arange(half_width).astype(F32)
    inverse_freq = jnp.exp(freq_index * (-2.0 * math.log(THETA) / width))
    angles = positions.astype(F32)[:, None] * inverse_freq[None, :]
    cosine, sine = jnp.cos(angles), jnp.sin(angles)
    return jnp.concatenate((cosine, cosine), 1), jnp.concatenate((-sine, sine), 1)


def rms_unit(values):
    inv_scale = lax.rsqrt(jnp.mean(values * values, -1, keepdims=True) + EPS)
    return (values * inv_scale, inv_scale)


def rms_back(grad_out, gain_vec, unit_vals, inv_scale):
    scaled_grad = grad_out * gain_vec
    return inv_scale * (
        scaled_grad - unit_vals * jnp.mean(scaled_grad * unit_vals, -1, keepdims=True)
    )


def matmul(left, right):
    return jnp.dot(left, right, preferred_element_type=F32)


def contract_rows(left, right):
    return lax.dot_general(left, right, (((0,), (0,)), ((), ())), preferred_element_type=F32)


def contract_cols(left, right):
    return lax.dot_general(left, right, (((1,), (1,)), ((), ())), preferred_element_type=F32)


BLOCK = 256


def turn(values, cosine, sine):
    return values * cosine + pltpu.roll(values, HD // 2, 1) * sine


def turn_back(values, cosine, sine):
    return values * cosine - pltpu.roll(values, HD // 2, 1) * sine


def unit_of(raw):
    inv_scale = lax.rsqrt(jnp.mean(raw * raw, -1, keepdims=True) + EPS)
    return raw * inv_scale, inv_scale


def heads_stacked(ref, rows, per_group):
    return jnp.concatenate([ref[rows, r * HD : (r + 1) * HD] for r in range(per_group)], 0)


def causal_mask(key_end, row_start, block, per_group):
    keys = lax.broadcasted_iota(jnp.int32, (key_end, per_group * block), 0)
    queries = lax.broadcasted_iota(jnp.int32, (key_end, per_group * block), 1)
    return keys <= row_start + (queries & (block - 1))


def attend_kernel(
    x_ref,
    wq_ref,
    wk_ref,
    wv_ref,
    cos_ref,
    sin_ref,
    gq_ref,
    gk_ref,
    heads_ref,
    qraw_ref,
    kraw_ref,
    qb_ref,
    kb_ref,
    vb_ref,
    lse_ref,
    *,
    per_group,
    block,
):
    length = x_ref.shape[0]
    scale_qk = 1.0 / math.sqrt(HD)
    for i in range(length // block):
        rows = slice(i * block, (i + 1) * block)
        x = x_ref[rows, :]
        cosine, sine = cos_ref[rows, :], sin_ref[rows, :]
        qraw = jnp.dot(x, wq_ref[...], preferred_element_type=F32)
        kraw = jnp.dot(x, wk_ref[...], preferred_element_type=F32)
        qraw_ref[rows, :] = qraw
        kraw_ref[rows, :] = kraw
        vb_ref[rows, :] = jnp.dot(x, wv_ref[...], preferred_element_type=F32).astype(BF)
        for r in range(per_group):
            cols = slice(r * HD, (r + 1) * HD)
            unit, _ = unit_of(qraw[:, cols])
            qb_ref[rows, cols] = turn(unit * gq_ref[...], cosine, sine).astype(BF)
        unit, _ = unit_of(kraw)
        kb_ref[rows, :] = turn(unit * gk_ref[...], cosine, sine).astype(BF)
        key_end = (i + 1) * block
        queries = heads_stacked(qb_ref, rows, per_group)
        scores = contract_cols(kb_ref[:key_end, :], queries) * scale_qk
        scores = jnp.where(causal_mask(key_end, i * block, block, per_group), scores, -jnp.inf)
        top = jnp.max(scores, 0, keepdims=True)
        shifted = jnp.exp(scores - top)
        total = jnp.sum(shifted, 0, keepdims=True)
        probs = (shifted * (1.0 / total)).astype(BF)
        out = contract_rows(vb_ref[:key_end, :], probs).T
        log_sum = top + jnp.log(total)
        for r in range(per_group):
            part = slice(r * block, (r + 1) * block)
            heads_ref[rows, r * HD : (r + 1) * HD] = out[part, :].astype(BF)
            lse_ref[r : r + 1, rows] = log_sum[:, part]


def attend_back_kernel(
    resid_ref,
    wo_ref,
    qb_ref,
    kb_ref,
    vb_ref,
    qraw_ref,
    kraw_ref,
    lse_ref,
    cos_ref,
    sin_ref,
    gq_ref,
    gk_ref,
    grad_ref,
    term_ref,
    key_acc,
    value_acc,
    *,
    per_group,
    block,
    groups,
):
    length = resid_ref.shape[0]
    scale_qk = 1.0 / math.sqrt(HD)
    group = pl.program_id(0)
    blocks = length // block

    @pl.when(group == 0)
    def _():
        term_ref[...] = jnp.zeros_like(term_ref)

    def column(index):
        return pl.ds(pl.multiple_of(index * HD, HD), HD)

    for i in reversed(range(blocks)):
        rows = slice(i * block, (i + 1) * block)
        key_end = (i + 1) * block
        grad = contract_cols(resid_ref[rows, :], wo_ref[...]).astype(BF)
        grads = jnp.concatenate(
            [grad[:, r * HD : (r + 1) * HD] for r in range(per_group)], 0
        )
        queries = heads_stacked(qb_ref, rows, per_group)
        keys, values = kb_ref[:key_end, :], vb_ref[:key_end, :]
        log_sum = jnp.concatenate([lse_ref[r : r + 1, rows] for r in range(per_group)], 1)
        scores = contract_cols(keys, queries) * scale_qk
        probs = jnp.where(
            causal_mask(key_end, i * block, block, per_group), jnp.exp(scores - log_sum), 0.0
        )
        grad_probs = contract_cols(values, grads)
        row_dot = jnp.sum(probs * grad_probs, 0, keepdims=True)
        grad_scores = (probs * (grad_probs - row_dot)).astype(BF)
        value_part = jnp.dot(probs.astype(BF), grads, preferred_element_type=F32)
        key_part = jnp.dot(grad_scores, queries, preferred_element_type=F32) * scale_qk
        if i == blocks - 1:
            value_acc[...] = value_part
            key_acc[...] = key_part
        else:
            value_acc[:key_end, :] += value_part
            key_acc[:key_end, :] += key_part
        grad_query = contract_rows(keys, grad_scores).T * scale_qk
        cosine, sine = cos_ref[rows, :], sin_ref[rows, :]
        for r in range(per_group):
            normed = turn_back(grad_query[r * block : (r + 1) * block, :], cosine, sine)
            unit, inv_scale = unit_of(qraw_ref[rows, r * HD : (r + 1) * HD])
            term_ref[0:1, :] += jnp.sum(normed * unit, 0, keepdims=True)
            grad_ref[rows, column(group * per_group + r)] = rms_back(
                normed, gq_ref[...], unit, inv_scale
            ).astype(BF)
    for i in range(blocks):
        rows = slice(i * block, (i + 1) * block)
        normed = turn_back(key_acc[rows, :], cos_ref[rows, :], sin_ref[rows, :])
        unit, inv_scale = unit_of(kraw_ref[rows, :])
        term_ref[1:2, :] += jnp.sum(normed * unit, 0, keepdims=True)
        grad_ref[rows, column(groups * per_group + group)] = rms_back(
            normed, gk_ref[...], unit, inv_scale
        ).astype(BF)
        grad_ref[rows, column(groups * (per_group + 1) + group)] = value_acc[rows, :].astype(BF)


def attend(rows_attn, full_attn, tables, gains, groups, per_group):
    length, width = rows_attn.shape
    block = min(length, BLOCK)
    heads = groups * per_group
    whole = lambda shape: pl.BlockSpec(shape, lambda g: (0, 0))
    wide = pl.BlockSpec((length, per_group * HD), lambda g: (0, g))
    narrow = pl.BlockSpec((length, HD), lambda g: (0, g))
    return pl.pallas_call(
        functools.partial(attend_kernel, per_group=per_group, block=block),
        name="attend",
        grid=(groups,),
        in_specs=[
            whole((length, width)),
            pl.BlockSpec((width, per_group * HD), lambda g: (0, g)),
            pl.BlockSpec((width, HD), lambda g: (0, heads + g)),
            pl.BlockSpec((width, HD), lambda g: (0, heads + groups + g)),
            whole((length, HD)),
            whole((length, HD)),
            whole((1, HD)),
            whole((1, HD)),
        ],
        out_specs=[
            wide,
            wide,
            narrow,
            wide,
            narrow,
            narrow,
            pl.BlockSpec((None, per_group, length), lambda g: (g, 0, 0)),
        ],
        out_shape=[
            jax.ShapeDtypeStruct((length, heads * HD), BF),
            jax.ShapeDtypeStruct((length, heads * HD), F32),
            jax.ShapeDtypeStruct((length, groups * HD), F32),
            jax.ShapeDtypeStruct((length, heads * HD), BF),
            jax.ShapeDtypeStruct((length, groups * HD), BF),
            jax.ShapeDtypeStruct((length, groups * HD), BF),
            jax.ShapeDtypeStruct((groups, per_group, length), F32),
        ],
        cost_estimate=pl.CostEstimate(
            flops=2 * length * width * (heads + 2 * groups) * HD + 3 * length * length * heads * HD,
            bytes_accessed=length * (heads + 2 * groups) * HD * 10,
            transcendentals=length * length * heads,
        ),
    )(rows_attn, full_attn, full_attn, full_attn, *tables, *gains)


def attend_back(rows_resid, full_out, out_column, saved, tables, gains, groups, per_group):
    length, width = rows_resid.shape
    qraw, kraw, qb, kb, vb, lse = saved
    block = min(length, BLOCK)
    heads = groups * per_group
    columns = (heads + 2 * groups) * HD
    whole = lambda shape: pl.BlockSpec(shape, lambda g: (0, 0))
    wide = pl.BlockSpec((length, per_group * HD), lambda g: (0, g))
    narrow = pl.BlockSpec((length, HD), lambda g: (0, g))
    return pl.pallas_call(
        functools.partial(attend_back_kernel, per_group=per_group, block=block, groups=groups),
        name="attend_back",
        grid=(groups,),
        in_specs=[
            whole((length, width)),
            pl.BlockSpec((per_group * HD, width), lambda g: (g, out_column)),
            wide,
            narrow,
            narrow,
            wide,
            narrow,
            pl.BlockSpec((None, per_group, length), lambda g: (g, 0, 0)),
            whole((length, HD)),
            whole((length, HD)),
            whole((1, HD)),
            whole((1, HD)),
        ],
        out_specs=[whole((length, columns)), whole((8, HD))],
        out_shape=[
            jax.ShapeDtypeStruct((length, columns), BF),
            jax.ShapeDtypeStruct((8, HD), F32),
        ],
        scratch_shapes=[pltpu.VMEM((length, HD), F32), pltpu.VMEM((length, HD), F32)],
        cost_estimate=pl.CostEstimate(
            flops=2 * length * width * heads * HD + 7 * length * length * heads * HD,
            bytes_accessed=length * columns * 10,
            transcendentals=length * length * heads,
        ),
    )(rows_resid, full_out, qb, kb, vb, qraw, kraw, lse, *tables, *gains)


def mlp_kernel(
    x_ref,
    cot_ref,
    wg_ref,
    wu_ref,
    wd_ref,
    *refs,
    steps,
):
    active_ref, gate_ref, up_ref, down_ref, normed_ref, down_acc, normed_acc = refs[-7:]
    step = pl.program_id(0)

    @pl.when(step == 0)
    def _():
        down_acc[...] = jnp.zeros_like(down_acc)
        normed_acc[...] = jnp.zeros_like(normed_acc)

    half = min(x_ref.shape[0], 256)
    for i in range(x_ref.shape[0] // half):
        rows = slice(i * half, (i + 1) * half)
        x = x_ref[rows, :]
        gate = jnp.dot(x, wg_ref[...], preferred_element_type=F32)
        up = jnp.dot(x, wu_ref[...], preferred_element_type=F32)
        grad_active = contract_cols(cot_ref[rows, :], wd_ref[...])
        sigmoid = 1.0 / (1.0 + jnp.exp(-gate))
        silu = gate * sigmoid
        active = (silu * up).astype(BF)
        grad_gate = (grad_active * up * sigmoid * (1.0 + gate * (1.0 - sigmoid))).astype(BF)
        grad_up = (grad_active * silu).astype(BF)
        active_ref[rows, :] = active
        gate_ref[rows, :] = grad_gate
        up_ref[rows, :] = grad_up
        down_acc[rows, :] += jnp.dot(active, wd_ref[...], preferred_element_type=F32)
        normed_acc[rows, :] += contract_cols(grad_gate, wg_ref[...]) + contract_cols(
            grad_up, wu_ref[...]
        )

    @pl.when(step == steps - 1)
    def _():
        down_ref[...] = down_acc[...].astype(down_ref.dtype)
        normed_ref[...] = normed_acc[...].astype(normed_ref.dtype)


def mlp(rows_x, rows_cot, part, parts, full_mlp, full_down, units, dtype, held=()):
    rows, width = rows_x.shape
    block = next(b for b in (384, 256, 128) if units % b == 0)
    steps = units // block
    whole = pl.BlockSpec((rows, width), lambda j: (0, 0))
    piece = pl.BlockSpec((rows, block), lambda j: (part, j))
    full = jax.ShapeDtypeStruct((rows * parts, units), BF)
    total = jax.ShapeDtypeStruct((rows, width), dtype)
    return pl.pallas_call(
        functools.partial(mlp_kernel, steps=steps),
        name="feed_forward",
        grid=(steps,),
        in_specs=[
            whole,
            whole,
            pl.BlockSpec((width, block), lambda j: (0, j)),
            pl.BlockSpec((width, block), lambda j: (0, steps + j)),
            pl.BlockSpec((block, width), lambda j: (j, 0)),
        ]
        + [pl.BlockSpec(memory_space=pl.ANY)] * len(held),
        out_specs=[piece, piece, piece, whole, whole],
        out_shape=[full, full, full, total, total],
        input_output_aliases={5 + i: i for i in range(len(held))},
        scratch_shapes=[pltpu.VMEM((rows, width), F32), pltpu.VMEM((rows, width), F32)],
        cost_estimate=pl.CostEstimate(
            flops=12 * rows * width * units,
            bytes_accessed=6 * width * units + 6 * rows * units,
            transcendentals=rows * units,
        ),
    )(rows_x, rows_cot, full_mlp, full_mlp, full_down, *held)


def all_sum(value, sizes):
    for axis, size in sizes:
        if size & (size - 1):
            value = lax.psum(value, axis)
            continue
        step = 1
        while step < size:
            value = value + lax.ppermute(value, axis, [(i, i ^ step) for i in range(size)])
            step *= 2
    return value


def pack_rows(shard, rows):
    count, width = shard.shape
    if 2 * count == 3 * rows and rows % 32 == 0:
        tail = shard[rows:]
        half = width // 2
        return jnp.concatenate(
            (shard[:rows], jnp.concatenate((tail[:, :half], tail[:, half:]), 0)), 1
        )
    return shard.reshape(rows, -1)


def unpack_rows(packed, parts, width):
    total, wide = packed.shape
    rows = total // parts
    if 2 * wide == 3 * width and rows % 32 == 0:
        blocks = packed.reshape(parts, rows, wide)
        tail = blocks[:, :, width:]
        tail = jnp.concatenate((tail[:, : rows // 2], tail[:, rows // 2 :]), 2)
        return jnp.concatenate((blocks[:, :, :width], tail), 1).reshape(-1, width)
    return packed.reshape(-1, width)


def pack_blocks(full, parts, rows):
    total, width = full.shape
    count = total // parts
    if 2 * count == 3 * rows and rows % 32 == 0:
        blocks = full.reshape(parts, count, width)
        tail = blocks[:, rows:]
        half = width // 2
        tail = jnp.concatenate((tail[:, :, :half], tail[:, :, half:]), 1)
        return jnp.concatenate((blocks[:, :rows], tail), 2).reshape(parts * rows, -1)
    return full.reshape(parts * rows, -1)


def make_local(n_dp, n_tensor):
    paired = n_tensor == 2

    def swap(value):
        return lax.ppermute(value, "tensor", [(0, 1), (1, 0)])

    def in_order(own, other):
        first = lax.axis_index("tensor") == 0
        return jnp.concatenate((jnp.where(first, own, other), jnp.where(first, other, own)), 0)

    def sequence_rows(own):
        if paired:
            return in_order(own, swap(own))
        return lax.all_gather(own, "tensor", axis=0, tiled=True)

    def scatter_rows(part, operand):
        if paired:
            half = operand.shape[0] // 2
            me = lax.axis_index("tensor")
            other_rows = lax.dynamic_slice_in_dim(operand, (1 - me) * half, half, 0)
            own_rows = lax.dynamic_slice_in_dim(operand, me * half, half, 0)
            got = swap(part(other_rows).astype(BF))
            return part(own_rows) + got.astype(F32)
        return sum_rows(part(operand).astype(BF))

    def sum_rows(value):
        return lax.psum_scatter(value, "tensor", scatter_dimension=0, tiled=True).astype(F32)

    def local(
        hidden_in,
        positions,
        gain_attention,
        gain_feedforward,
        gain_query,
        gain_key,
        query_proj,
        key_proj,
        value_proj,
        out_proj,
        gate_proj,
        up_proj,
        down_proj,
        cotangent,
    ):
        width = hidden_in.shape[1]
        heads_here = query_proj.shape[1] // HD
        groups_here = key_proj.shape[1] // HD
        per_group = heads_here // groups_here
        width_query = heads_here * HD
        width_key = groups_here * HD
        width_qkv = width_query + 2 * width_key
        units = gate_proj.shape[1]
        shard_rows = query_proj.shape[0]

        shard_attn = jnp.concatenate(
            (query_proj, key_proj, value_proj, out_proj.reshape(shard_rows, -1)), 1
        )
        shard_mlp = jnp.concatenate((gate_proj, up_proj, pack_rows(down_proj, shard_rows)), 1)
        full_attn = lax.all_gather(shard_attn, "dp", axis=0, tiled=True)
        full_mlp = lax.all_gather(shard_mlp, "dp", axis=0, tiled=True)
        full_down = unpack_rows(full_mlp[:, 2 * units :], n_dp, width)
        if out_proj.shape == (shard_rows, width) and width_qkv % width == 0:
            out_source, out_column = full_attn, width_qkv // width
            full_out = full_attn[:, width_qkv:]
        else:
            full_out = full_attn[:, width_qkv:].reshape(-1, width)
            out_source, out_column = full_out, 0

        hidden_f = hidden_in.astype(F32)
        unit_attn, scale_attn = rms_unit(hidden_f)
        rows_hidden = sequence_rows(hidden_in)
        rows_attn = (rms_unit(rows_hidden.astype(F32))[0] * gain_attention).astype(BF)
        tables = rotary_tables(positions, HD)
        gains = (gain_query.reshape(1, HD), gain_key.reshape(1, HD))
        if paired:
            other_cot = swap(cotangent)
        else:
            rows_cot = lax.all_gather(cotangent, "tensor", axis=0, tiled=True)

        heads_b, *saved = attend(rows_attn, full_attn, tables, gains, groups_here, per_group)
        qraw, kraw, qb, kb, vb, lse = saved
        resid = hidden_f + scatter_rows(lambda h: matmul(h, full_out), heads_b)
        unit_mlp, scale_mlp = rms_unit(resid)
        normed_mlp = (unit_mlp * gain_feedforward).astype(BF)
        if paired:
            other_mlp = swap(normed_mlp)
            run = functools.partial(
                mlp, parts=2, full_mlp=full_mlp, full_down=full_down, units=units
            )
            *held, sent_down, sent_normed = run(other_mlp, other_cot, 1, dtype=BF)
            got_normed = swap(sent_normed)
            active_b, grad_gate_b, grad_up_b, own_down, own_normed = run(
                normed_mlp, cotangent, 0, dtype=F32, held=tuple(held)
            )
            grad_normed_mlp = own_normed + got_normed.astype(F32)
            rows_mlp = jnp.concatenate((normed_mlp, other_mlp), 0)
            rows_cot = jnp.concatenate((cotangent, other_cot), 0)
        else:
            rows_mlp = lax.all_gather(normed_mlp, "tensor", axis=0, tiled=True)
            active_b, grad_gate_b, grad_up_b, sent_down, sent_normed = mlp(
                rows_mlp, rows_cot, 0, 1, full_mlp, full_down, units, BF
            )
            grad_normed_mlp = sum_rows(sent_normed)
        grad_mlp_w = jnp.concatenate(
            (
                contract_rows(rows_mlp, grad_gate_b).astype(BF),
                contract_rows(rows_mlp, grad_up_b).astype(BF),
                pack_blocks(contract_rows(active_b, rows_cot).astype(BF), n_dp, shard_rows),
            ),
            1,
        )
        sent_mlp = lax.psum_scatter(grad_mlp_w, "dp", scatter_dimension=0, tiled=True)

        term_feedforward = jnp.sum(grad_normed_mlp * unit_mlp, 0)
        grad_resid = cotangent.astype(F32) + rms_back(
            grad_normed_mlp, gain_feedforward, unit_mlp, scale_mlp
        )
        rows_resid = sequence_rows(grad_resid.astype(BF))
        rows_resid, sent_down, grad_mlp_w = lax.optimization_barrier(
            (rows_resid, sent_down, grad_mlp_w)
        )
        if paired:
            output_b = (resid + own_down + swap(sent_down).astype(F32)).astype(BF)
        else:
            output_b = (resid + sum_rows(sent_down)).astype(BF)

        grad_qkv_b, terms_qk = attend_back(
            rows_resid,
            out_source,
            out_column,
            (qraw, kraw, qb, kb, vb, lse),
            tables,
            gains,
            groups_here,
            per_group,
        )
        grad_attn_w = jnp.concatenate(
            (
                contract_rows(rows_attn, grad_qkv_b).astype(BF),
                contract_rows(heads_b, rows_resid).astype(BF).reshape(width, -1),
            ),
            1,
        )
        grad_attn_w, sent_mlp = lax.optimization_barrier((grad_attn_w, sent_mlp))
        sent_attn = lax.psum_scatter(grad_attn_w, "dp", scatter_dimension=0, tiled=True)
        grad_normed_attn = scatter_rows(
            lambda g: contract_cols(g, full_attn[:, :width_qkv]), grad_qkv_b
        )
        term_attention = jnp.sum(grad_normed_attn * unit_attn, 0)
        grad_hidden = grad_resid + rms_back(
            grad_normed_attn, gain_attention, unit_attn, scale_attn
        )
        terms = all_sum(
            jnp.concatenate(
                (term_attention, term_feedforward, terms_qk[0], terms_qk[1])
            ).reshape(-1, HD),
            (("tensor", n_tensor), ("dp", n_dp)),
        ).reshape(-1)
        sent_attn = sent_attn.astype(F32)
        sent_mlp = sent_mlp.astype(F32)
        return (
            output_b,
            grad_hidden,
            terms[:width],
            terms[width : 2 * width],
            terms[2 * width : 2 * width + HD],
            terms[2 * width + HD :],
            sent_attn[:, :width_query],
            sent_attn[:, width_query : width_query + width_key],
            sent_attn[:, width_query + width_key : width_qkv],
            sent_attn[:, width_qkv:].reshape(out_proj.shape),
            sent_mlp[:, :units],
            sent_mlp[:, units : 2 * units],
            unpack_rows(sent_mlp[:, 2 * units :], 1, width),
        )

    return local


def solution(mesh):
    rows = P(("dp", "tensor"), None)
    cut = P("dp", "tensor")
    stacked = P(("tensor", "dp"), None)
    return jax.shard_map(
        make_local(mesh.shape["dp"], mesh.shape["tensor"]),
        mesh=mesh,
        in_specs=(
            rows,
            P("dp"),
            P(),
            P(),
            P(),
            P(),
            cut,
            cut,
            cut,
            stacked,
            cut,
            cut,
            stacked,
            rows,
        ),
        out_specs=(rows, rows, P(), P(), P(), P(), cut, cut, cut, stacked, cut, cut, stacked),
        check_vma=False,
    )
```

time: 643 us -> 451 us (0.70)
  matrix products: 152 us -> 45.5 us
  Pallas kernels: 0 us -> 94.8 us
  other arithmetic: 101 us -> 33.2 us
  local copies, waits for them, and re-layouts: 70.6 us -> 14.8 us
  waiting for transfers between devices: 274 us -> 226 us
    pallas_call x0 -> x4, Pallas kernels: none -> 94.8 us  [the longest x2 39.2 us: mlp(): pl.pallas_call(functools.partial(mlp_kernel, steps=steps), name='feed_for...]
    reduce_scatter x1, waiting for transfers between devices: 97.4 us -> 9.05 us  [local(): lax.psum_scatter(grad_mlp_w, 'dp', scatter_dimension=0, tiled=True)]
    dot_general x12 -> x0, matrix products: 54 us -> none  [the longest x2 13.1 us: attend_back(): jnp.einsum('qgrd,kgd->grqk', grad_block, value_b[:key_end], preferred_ele...]
    dot_general x7 -> x2, matrix products: 40.6 us -> 6.83 us  [matmul(): return jnp.dot(left, right, preferred_element_type=F32)]
    reduce_sum x7 -> x1, other arithmetic: 34.6 us -> 2.47 us  [local(): term_feedforward = jnp.sum(grad_normed_mlp * unit_mlp, 0)]
    reduce_scatter x1, waiting for transfers between devices: 0.01 us -> 23.9 us  [local(): lax.psum_scatter(grad_attn_w, 'dp', scatter_dimension=0, tiled=True)]
    all_gather x1, waiting for transfers between devices: 0.01 us -> 20.4 us  [local(): full_mlp = lax.all_gather(shard_mlp, 'dp', axis=0, tiled=True)]
    unnamed x213 -> x30, local copies, waits for them, and re-layouts: 23.4 us -> 4.03 us
  transfers between devices with their start and end apart: 17 -> 17, of which waited for: 13 -> 15; matrix products, arithmetic and copies ran while one was open for 26% -> 14% of each run, Pallas kernels for 0% -> 12%
where the time goes in v2:
time: 451 us; the launch traced here: 447 us
  waiting for transfers between devices  226 us (50%)
  Pallas kernels  94.8 us (21%)
  matrix products  45.5 us (10%)
  other arithmetic  33.2 us (7%)
  starting transfers between devices  18.8 us (4%)
  local copies, waits for them, and re-layouts  14.8 us (3%)
  between operations  14.3 us (3%)
    ppermute x8, waiting for transfers between devices, swap(): return lax.ppermute(value, 'tensor', [(0, 1), (1, 0)])  135 us
    pallas_call x2, Pallas kernels, mlp(): pl.pallas_call(functools.partial(mlp_kernel, steps=steps), name='feed_for...  39.2 us
    all_gather x1, waiting for transfers between devices, local(): full_attn = lax.all_gather(shard_attn, 'dp', axis=0, tiled=True)  31.9 us
    pallas_call x1, Pallas kernels, attend_back(): pl.pallas_call(functools.partial(attend_back_kernel, per_group=per_group,...  29.8 us
    dot_general x5, matrix products, contract_rows(): lax.dot_general(left, right, (((0,), (0,)), ((), ())), preferred_element_...  28.2 us
    pallas_call x1, Pallas kernels, attend(): pl.pallas_call(functools.partial(attend_kernel, per_group=per_group, bloc...  25.8 us
    reduce_scatter x1, waiting for transfers between devices, local(): lax.psum_scatter(grad_attn_w, 'dp', scatter_dimension=0, tiled=True)  23.9 us
    all_gather x1, waiting for transfers between devices, local(): full_mlp = lax.all_gather(shard_mlp, 'dp', axis=0, tiled=True)  20.4 us
  transfers between devices with their start and end apart: 17, of which 15 were waited for; matrix products, arithmetic and copies ran while one was open for 14% of the time, Pallas kernels for 12%

profile of v2, /device:TPU:0, one launch (start us, length us, event | category | flops | bytes accessed | tf_op | source)
XLA Modules:
  0.0 447.1 jit_solution(3481992221678489603)
XLA Ops:
  7.2 1.9 pad_maximum_fusion.9
  10.9 1.9 maximum_maximum_fusion.2
  12.8 3.1 collective-permute-start
  15.9 1.9 fusion.41
  19.2 20.0 %collective-permute-done = bf16[512,1024]{1,0:T(8,128)(2,1)} collective-permute-done((bf16[512,1024]{1,0:T(8,128)(2,1)S(1)}, bf16[512,1024]{1,0:T(8,128)(2,1)}, u32[]{:S(2)}, u32[]{:S(2)}) %collective-permute-start) | collective-permute-done | bytes 1048608 | tf_op jit(solution)/shard_map/ppermute | solution.py:422
  41.2 1.9 fusion.2.x_ref
  43.1 31.9 %all-gather.3.cloned.1.call-done.wq_ref.wk_ref.wv_ref.wo_ref = bf16[1024,3072]{1,0:T(8,128)(2,1)} async-done(((bf16[64,3072]{1,0:T(8,128)(2,1)}), bf16[1024,3072]{1,0:T(8,128)(2,1)}) %all-gather.3.cloned.1.call-update) | async-done | bytes 6291472 | tf_op jit(solution)/shard_map/all_gather | solution.py:476
  75.0 25.8 %attend.1 = (bf16[1024,1024]{1,0:T(8,128)(2,1)}, f32[1024,1024]{1,0:T(8,128)}, f32[1024,512]{1,0:T(8,128)}, bf16[1024,1024]{1,0:T(8,128)(2,1)}, bf16[1024,512]{1...) custom-call(bf16[1024,1024]{1,0:T(8,128)(2,1)} %fusion.2.x_ref, ...), custom_call_target="tpu_custom_call" | custom-call | flops 7516192768 | bytes 20971520 | tf_op jit(solution)/shard_map/attend/pallas_call | solution.py:216
  100.8 3.2 fusion.34
  104.0 1.5 collective-permute-start.1
  106.1 24.1 %collective-permute-done.1 = bf16[512,1024]{1,0:T(8,128)(2,1)} collective-permute-done((bf16[512,1024]{1,0:T(8,128)(2,1)S(1)}, bf16[512,1024]{1,0:T(8,128)(2,1)}, u32[]{:S(2)}, u32[]{:S(2)}) %collective-permute-start.1) | collective-permute-done | bytes 1048608 | tf_op jit(solution)/shard_map/ppermute | solution.py:422
  130.2 3.7 multiply_reduce_fusion.2
  136.6 20.4 %all-gather.5.cloned.1.call-done.wg_ref.wu_ref = bf16[1024,4608]{1,0:T(8,128)(2,1)} async-done(((bf16[64,4608]{1,0:T(8,128)(2,1)}), bf16[1024,4608]{1,0:T(8,128)(2,1)}) %all-gather.5.cloned.1.call-update) | async-done | bytes 9437200 | tf_op jit(solution)/shard_map/all_gather | solution.py:477
  156.9 2.1 slice.142
  159.4 1.9 maximum_maximum_fusion
  161.2 13.2 %collective-permute-done.2.x_ref = bf16[512,1024]{1,0:T(8,128)(2,1)} collective-permute-done((bf16[512,1024]{1,0:T(8,128)(2,1)}, bf16[512,1024]{1,0:T(8,128)(2,1)}, u32[]{:S(2)}, u32[]{:S(2)}) %collective-permute-start.2) | collective-permute-done | bytes 1048608 | tf_op jit(solution)/shard_map/ppermute | solution.py:422
  174.4 19.5 %feed_forward.2 = (bf16[1024,1536]{1,0:T(8,128)(2,1)}, bf16[1024,1536]{1,0:T(8,128)(2,1)}, bf16[1024,1536]{1,0:T(8,128)(2,1)}, bf16[512,1024]{1,0:T(8,128)(2,1)}, bf16[512,1024]{1,0:T(8,128)(2,1)}) custom-call(bf16[512,1024]{1,0:T(8,128)(2,1)} %collective-permute-done.2.x_ref, bf16[512,1024]{1,0:T(8,128)(2,1)} %collective-permute-done.3.cot_ref, ...), custom_call_target="tpu_custom_call" | custom-call | flops 9663676416 | bytes 14155776 | tf_op jit(solution)/shard_map/feed_forward/pallas_call | solution.py:348
  193.9 19.7 %feed_forward.3 = (bf16[1024,1536]{1,0:T(8,128)(2,1)}, bf16[1024,1536]{1,0:T(8,128)(2,1)}, bf16[1024,1536]{1,0:T(8,128)(2,1)}, f32[512,1024]{1,0:T(8,128)}, f32[512,1024]{1,0:T(8,128)}) custom-call(bf16[512,1024]{1,0:T(8,128)(2,1)} %multiply_convert_fusion.x_ref, ...), custom_call_target="tpu_custom_call", output_to_operand_aliasing={{0}: (5, {}), {1}: (6, {}), {2}: (7, {})} | custom-call | flops 9663676416 | bytes 14155776 | tf_op jit(solution)/shard_map/feed_forward/pallas_call | solution.py:348
  213.6 5.9 %convolution_convert_fusion = bf16[1536,1024]{1,0:T(8,128)(2,1)S(1)} fusion(bf16[1024,1536]{1,0:T(8,128)(2,1)} %get-tuple-element.46, bf16[512,1024]{1,0:T(8,128)(2,1)} %collective-permute-done.3.cot_ref, bf16[512,1024]{1,0:T(8,128)(2,1)} %cot_ref.1), kind=kOutput, calls=%fused_computation.7 | convolution fusion | flops 3226992640 | bytes 8388608 | tf_op jit(solution)/shard_map/dot_general | solution.py:44
  220.2 1.6 copy-done.11
  221.8 5.6 %convolution_convert_fusion.2 = bf16[1024,1536]{1,0:T(8,128)(2,1)S(1)} fusion(bf16[1024,1536]{1,0:T(8,128)(2,1)S(1)} %copy-done.11, bf16[512,1024]{1,0:T(8,128)(2,1)} %collective-permute-done.2.x_ref, bf16[512,1024]{1,0:T(8,128)(2,1)} %multiply_convert_fusion.x_ref), kind=kOutput, calls=%fused_computation.9 | convolution fusion | flops 3226992640 | bytes 8388608 | tf_op jit(solution)/shard_map/dot_general | solution.py:44
  227.5 5.4 %convolution_convert_fusion.1 = bf16[1024,1536]{1,0:T(8,128)(2,1)S(1)} fusion(bf16[1024,1536]{1,0:T(8,128)(2,1)S(1)} %copy-done.12, bf16[512,1024]{1,0:T(8,128)(2,1)} %collective-permute-done.2.x_ref, bf16[512,1024]{1,0:T(8,128)(2,1)} %multiply_convert_fusion.x_ref), kind=kOutput, calls=%fused_computation.8 | convolution fusion | flops 3226992640 | bytes 8388608 | tf_op jit(solution)/shard_map/dot_general | solution.py:44
  232.9 5.2 %pad_maximum_fusion = bf16[1024,4608]{1,0:T(8,128)(2,1)} fusion(bf16[1024,1536]{1,0:T(8,128)(2,1)S(1)} %bitcast.35, bf16[1024,1536]{1,0:T(8,128)(2,1)S(1)} %convolution_convert_fusion.1, bf16[1024,1536]{1,0:T(8,128)(2,1)S(1)} %convolution_convert_fusion.2), kind=kLoop, calls=%fused_computation | loop fusion | flops 28311552 | bytes 18874368 | tf_op jit(solution)/shard_map/concatenate | solution.py:521
  238.1 1.5 collective-permute-start.4
  239.6 23.2 %collective-permute-done.4 = bf16[512,1024]{1,0:T(8,128)(2,1)S(1)} collective-permute-done((bf16[512,1024]{1,0:T(8,128)(2,1)}, bf16[512,1024]{1,0:T(8,128)(2,1)S(1)}, u32[]{:S(2)}, u32[]{:S(2)}) %collective-permute-start.4) | collective-permute-done | bytes 1048608 | tf_op jit(solution)/shard_map/ppermute | solution.py:422
  262.8 2.5 multiply_reduce_fusion
  265.3 3.3 fusion.50
  270.1 22.1 %collective-permute-done.5 = bf16[512,1024]{1,0:T(8,128)(2,1)S(1)} collective-permute-done((bf16[512,1024]{1,0:T(8,128)(2,1)S(1)}, bf16[512,1024]{1,0:T(8,128)(2,1)S(1)}, u32[]{:S(2)}, u32[]{:S(2)}) %collective-permute-start.5) | collective-permute-done | bytes 1048608 | tf_op jit(solution)/shard_map/ppermute | solution.py:422
  292.5 2.2 copy-done.14
  294.7 3.7 convolution_convert_fusion.4
  298.5 29.8 %attend_back.1 = (bf16[1024,2048]{1,0:T(8,128)(2,1)}, f32[8,128]{1,0:T(8,128)}) custom-call(bf16[1024,1024]{1,0:T(8,128)(2,1)} %copy-done.5, bf16[1024,3072]{1,0:T(8,128)(2,1)} %all-gather.3.cloned.1.call-done.wq_ref.wk_ref.wv_ref.wo_ref, bf16[1024,1024]{1,0:T(8,128)(2,1)} %get-tuple-element.49.qb_ref, bf16[1024,512]{1,0:T(8,128)(2,1)} %get-tuple-element.50.kb_ref, ...), custom_call_target="tpu_custom_call" | custom-call | flops 9663676416 | bytes 20971520 | tf_op jit(solution)/shard_map/attend_back/pallas_call | solution.py:265
  328.3 7.5 %convolution_convert_fusion.3 = bf16[1024,2048]{1,0:T(8,128)(2,1)S(1)} fusion(bf16[1024,1024]{1,0:T(8,128)(2,1)} %fusion.2.x_ref, bf16[1024,2048]{1,0:T(8,128)(2,1)} %get-tuple-element.55), kind=kOutput, calls=%fused_computation.10 | convolution fusion | flops 4297064448 | bytes 10485760 | tf_op jit(solution)/shard_map/dot_general | solution.py:44
  335.9 3.2 pad_maximum_fusion.1
  339.1 9.1 %reduce-scatter.3.cloned.1.call-done = bf16[64,4608]{1,0:T(8,128)(2,1)} async-done(((bf16[1024,4608]{1,0:T(8,128)(2,1)}), bf16[64,4608]{1,0:T(8,128)(2,1)}) %reduce-scatter.3.cloned.1.call-update) | async-done | bytes 589840 | tf_op jit(solution)/shard_map/reduce_scatter | solution.py:529
  348.2 5.3 %fusion.29 = bf16[512,1024]{1,0:T(8,128)(2,1)S(1)} fusion(bf16[1024,3072]{1,0:T(8,128)(2,1)} %all-gather.3.cloned.1.call-done.wq_ref.wk_ref.wv_ref.wo_ref, bf16[1024,2048]{1,0:T(8,128)(2,1)} %get-tuple-element.55, s32[]{:T(128)S(6)} %select_n.32), kind=kOutput, calls=%fused_computation.50 | convolution fusion | flops 2148007936 | bytes 7340036 | tf_op jit(solution)/shard_map/dot_general | solution.py:48
  356.1 22.1 %collective-permute-done.7 = bf16[512,1024]{1,0:T(8,128)(2,1)S(1)} collective-permute-done((bf16[512,1024]{1,0:T(8,128)(2,1)S(1)}, bf16[512,1024]{1,0:T(8,128)(2,1)S(1)}, u32[]{:S(2)}, u32[]{:S(2)}) %collective-permute-start.7) | collective-permute-done | bytes 1048608 | tf_op jit(solution)/shard_map/ppermute | solution.py:422
  378.2 5.1 %fusion.14 = (f32[1024]{0:T(1024)S(1)}, f32[512]{0:T(512)S(1)}, f32[512,1024]{1,0:T(8,128)S(1)}) fusion(bf16[512,1024]{1,0:T(8,128)(2,1)S(1)} %copy-done, f32[512]{0:T(512)S(1)} %add_rsqrt_fusion.1, f32[1024]{0:T(1024)S(1)} %copy-done.8, bf16[512,1024]{1,0:T(8,128)(2,1)S(1)} %collective-permute-done.7, ...), kind=kOutput, calls=%fused_computation.27 | convolution fusion | flops 2152200704 | bytes 10498052 | tf_op jit(solution)/shard_map/dot_general | solution.py:48
  383.3 1.5 collective-permute-start.8
  385.4 1.8 collective-permute-done.8
  388.4 1.5 collective-permute-start.10
  389.9 2.6 collective-permute-done.10
  394.0 1.9 fusion.13
  396.2 2.3 collective-permute-start.12
  398.6 9.9 %collective-permute-done.6 = bf16[512,1024]{1,0:T(8,128)(2,1)S(1)} collective-permute-done((bf16[512,1024]{1,0:T(8,128)(2,1)S(1)}, bf16[512,1024]{1,0:T(8,128)(2,1)S(1)}, u32[]{:S(2)}, u32[]{:S(2)}) %collective-permute-start.6) | collective-permute-done | bytes 1048608 | tf_op jit(solution)/shard_map/ppermute | solution.py:422
  408.4 1.6 add_convert_fusion
  413.1 23.9 %reduce-scatter.5.cloned.1.call-done = bf16[64,3072]{1,0:T(8,128)(2,1)} async-done(((bf16[1024,3072]{1,0:T(8,128)(2,1)}), bf16[64,3072]{1,0:T(8,128)(2,1)}) %reduce-scatter.5.cloned.1.call-update) | async-done | bytes 393232 | tf_op jit(solution)/shard_map/reduce_scatter | solution.py:562
  436.9 1.8 fusion.55
  438.7 1.6 fusion.56
  (83 shorter events, 20.5 us)
Async XLA Ops:
  7.2 5.7 %copy-start = (bf16[512,1024]{1,0:T(8,128)(2,1)S(1)}, bf16[512,1024]{1,0:T(8,128)(2,1)}, u32[]{:S(2)}) copy-start(bf16[512,1024]{1,0:T(8,128)(2,1)} %param.14) | copy-start | bytes 3145732
  7.2 8.7 %copy-start.9 = (s32[1024]{0:T(1024)S(1)}, s32[1024]{0:T(1024)}, u32[]{:S(2)}) copy-start(s32[1024]{0:T(1024)} %param.15) | copy-start | bytes 12292
  7.2 67.8 %all-gather.3.cloned.1.call-start = ((), (), s32[]{:S(2)}) async-start(), calls=%async_computation.2 | async-start | bytes 6684672 | tf_op jit(solution)/shard_map/all_gather | solution.py:476
  9.2 147.8 %all-gather.5.cloned.1.call-start = ((), (), s32[]{:S(2)}) async-start(), calls=%async_computation.3 | async-start | bytes 10027008 | tf_op jit(solution)/shard_map/all_gather | solution.py:477
  12.8 335.3 %reduce-scatter.3.cloned.1.call-start = ((), (), s32[]{:S(2)}) async-start(), calls=%async_computation.4 | async-start | bytes 10027008 | tf_op jit(solution)/shard_map/reduce_scatter | solution.py:529
  12.8 26.3 %collective-permute-start = (bf16[512,1024]{1,0:T(8,128)(2,1)S(1)}, bf16[512,1024]{1,0:T(8,128)(2,1)}, u32[]{:S(2)}, u32[]{:S(2)}) collective-permute-start(bf16[512,1024]{1,0:T(8,128)(2,1)S(1)} %copy-done), channel_id=1, source_target_pairs={{0,1},{1,0},{2,3},{3,2},{4,5},{5,4},{6,7},{7,6},{8,9},{9,8},{10,11... | collective-permute-start | bytes 3145736 | tf_op jit(solution)/shard_map/ppermute | solution.py:422
  40.5 0.7 copy-start.8
  104.0 26.2 %collective-permute-start.1 = (bf16[512,1024]{1,0:T(8,128)(2,1)S(1)}, bf16[512,1024]{1,0:T(8,128)(2,1)}, u32[]{:S(2)}, u32[]{:S(2)}) collective-permute-start(bf16[512,1024]{1,0:T(8,128)(2,1)S(1)} %fusion.34), channel_id=1, source_target_pairs={{0,1},{1,0},{2,3},{3,2},{4,5},{5,4},{6,7},{7,6},{8,9},{9,8},{10,11... | collective-permute-start | bytes 3145736 | tf_op jit(solution)/shard_map/ppermute | solution.py:422
  105.5 55.7 %collective-permute-start.3 = (bf16[512,1024]{1,0:T(8,128)(2,1)}, bf16[512,1024]{1,0:T(8,128)(2,1)}, u32[]{:S(2)}, u32[]{:S(2)}) collective-permute-start(bf16[512,1024]{1,0:T(8,128)(2,1)} %cot_ref.1), channel_id=1, source_target_pairs={{0,1},{1,0},{2,3},{3,2},{4,5},{5,4},{6,7},{7,6},{8,9},{9,8},{10,11... | collective-permute-start | bytes 3145736 | tf_op jit(solution)/shard_map/ppermute | solution.py:422
  106.1 27.8 %copy-start.7 = (f32[1024]{0:T(1024)S(1)}, f32[1024]{0:T(1024)}, u32[]{:S(2)}) copy-start(f32[1024]{0:T(1024)} %param.17) | copy-start | bytes 12292
  135.1 39.3 %collective-permute-start.2 = (bf16[512,1024]{1,0:T(8,128)(2,1)}, bf16[512,1024]{1,0:T(8,128)(2,1)}, u32[]{:S(2)}, u32[]{:S(2)}) collective-permute-start(bf16[512,1024]{1,0:T(8,128)(2,1)} %multiply_convert_fusion.x_ref), channel_id=1, source_target_pairs={{0,1},{1,0},{2,3},{3,2},{4,5},{5,4},{6,7},{7,6},{8,9},{9,8},{10,11... | collective-permute-start | bytes 3145736 | tf_op jit(solution)/shard_map/ppermute | solution.py:422
  219.9 1.9 copy-start.11
  221.8 5.7 %copy-start.12 = (bf16[1024,1536]{1,0:T(8,128)(2,1)S(1)}, bf16[1024,1536]{1,0:T(8,128)(2,1)}, u32[]{:S(2)}) copy-start(bf16[1024,1536]{1,0:T(8,128)(2,1)} %get-tuple-element.45) | copy-start | bytes 9437188
  238.0 198.9 %reduce-scatter.5.cloned.1.call-start = ((), (), s32[]{:S(2)}) async-start(), calls=%async_computation.5 | async-start | bytes 6684672 | tf_op jit(solution)/shard_map/reduce_scatter | solution.py:562
  238.1 24.7 %collective-permute-start.4 = (bf16[512,1024]{1,0:T(8,128)(2,1)}, bf16[512,1024]{1,0:T(8,128)(2,1)S(1)}, u32[]{:S(2)}, u32[]{:S(2)}) collective-permute-start(bf16[512,1024]{1,0:T(8,128)(2,1)} %get-tuple-element.42), channel_id=1, source_target_pairs={{0,1},{1,0},{2,3},{3,2},{4,5},{5,4},{6,7},{7,6},{8,9},{9,8},{10,11... | collective-permute-start | bytes 3145736 | tf_op jit(solution)/shard_map/ppermute | solution.py:422
  262.8 2.5 copy-start.1
  268.6 23.6 %collective-permute-start.5 = (bf16[512,1024]{1,0:T(8,128)(2,1)S(1)}, bf16[512,1024]{1,0:T(8,128)(2,1)S(1)}, u32[]{:S(2)}, u32[]{:S(2)}) collective-permute-start(bf16[512,1024]{1,0:T(8,128)(2,1)S(1)} %get-tuple-element.63), channel_id=1, source_target_pairs={{0,1},{1,0},{2,3},{3,2},{4,5},{5,4},{6,7},{7,6},{8,9},{9,8},{10,11... | collective-permute-start | bytes 3145736 | tf_op jit(solution)/shard_map/ppermute | solution.py:422
  292.3 2.4 copy-start.14
  292.5 5.9 %copy-start.5 = (bf16[1024,1024]{1,0:T(8,128)(2,1)}, bf16[1024,1024]{1,0:T(8,128)(2,1)S(1)}, u32[]{:S(2)}) copy-start(bf16[1024,1024]{1,0:T(8,128)(2,1)S(1)} %pad_maximum_fusion.3.resid_ref) | copy-start | bytes 6291460
  328.3 7.6 %copy-start.6 = (bf16[1024,1024]{1,0:T(8,128)(2,1)S(1)}, bf16[1024,1024]{1,0:T(8,128)(2,1)}, u32[]{:S(2)}) copy-start(bf16[1024,1024]{1,0:T(8,128)(2,1)} %convolution_convert_fusion.4) | copy-start | bytes 6291460
  348.2 30.0 %copy-start.13 = (bf16[1024,2048]{1,0:T(8,128)(2,1)S(1)}, bf16[1024,2048]{1,0:T(8,128)(2,1)}, u32[]{:S(2)}) copy-start(bf16[1024,2048]{1,0:T(8,128)(2,1)} %get-tuple-element.55) | copy-start | bytes 12582916
  353.5 24.7 %collective-permute-start.7 = (bf16[512,1024]{1,0:T(8,128)(2,1)S(1)}, bf16[512,1024]{1,0:T(8,128)(2,1)S(1)}, u32[]{:S(2)}, u32[]{:S(2)}) collective-permute-start(bf16[512,1024]{1,0:T(8,128)(2,1)S(1)} %fusion.29), channel_id=1, source_target_pairs={{0,1},{1,0},{2,3},{3,2},{4,5},{5,4},{6,7},{7,6},{8,9},{9,8},{10,11... | collective-permute-start | bytes 3145736 | tf_op jit(solution)/shard_map/ppermute | solution.py:422
  356.1 28.7 %copy-start.10 = (bf16[512,1024]{1,0:T(8,128)(2,1)S(1)}, bf16[512,1024]{1,0:T(8,128)(2,1)}, u32[]{:S(2)}) copy-start(bf16[512,1024]{1,0:T(8,128)(2,1)} %get-tuple-element.47) | copy-start | bytes 3145732
  356.1 37.9 %copy-start.2 = (f32[512,1024]{1,0:T(8,128)S(1)}, f32[512,1024]{1,0:T(8,128)}, u32[]{:S(2)}) copy-start(f32[512,1024]{1,0:T(8,128)} %get-tuple-element.64) | copy-start | bytes 6291460
  383.3 3.9 collective-permute-start.8
  384.8 23.6 %collective-permute-start.6 = (bf16[512,1024]{1,0:T(8,128)(2,1)S(1)}, bf16[512,1024]{1,0:T(8,128)(2,1)S(1)}, u32[]{:S(2)}, u32[]{:S(2)}) collective-permute-start(bf16[512,1024]{1,0:T(8,128)(2,1)S(1)} %copy-done.10), channel_id=1, source_target_pairs={{0,1},{1,0},{2,3},{3,2},{4,5},{5,4},{6,7},{7,6},{8,9},{9,8},{10,11... | collective-permute-start | bytes 3145736 | tf_op jit(solution)/shard_map/ppermute | solution.py:422
  387.2 1.2 collective-permute-start.9
  388.4 4.1 collective-permute-start.10
  392.5 3.7 collective-permute-start.11
  394.0 14.4 %copy-start.4 = (f32[512,1024]{1,0:T(8,128)S(1)}, f32[512,1024]{1,0:T(8,128)}, u32[]{:S(2)}) copy-start(f32[512,1024]{1,0:T(8,128)} %get-tuple-element.40) | copy-start | bytes 6291460
  396.2 13.8 %collective-permute-start.12 = (f32[18,128]{1,0:T(8,128)S(1)}, f32[18,128]{1,0:T(8,128)S(1)}, u32[]{:S(2)}, u32[]{:S(2)}) collective-permute-start(f32[18,128]{1,0:T(8,128)S(1)} %add.95), channel_id=1, source_target_pairs={{0,16},{2,18},{4,20},{6,22},{8,24},{10,26},{12,28},{14,30},{16,0},... | collective-permute-start | bytes 27656 | tf_op jit(solution)/shard_map/ppermute | solution.py:379
  408.4 2.7 copy-start.3
Sparse Core Ops, SparseCore 0:
  10.9 64.1 all-gather.2
  77.3 79.5 all-gather.4
  238.2 109.9 reduce-scatter.2
  351.9 84.9 reduce-scatter.4

commit v3 on v2

--- a/solution.py
+++ b/solution.py
@@ -7,6 +7,7 @@
 from jax.experimental import pallas as pl
 from jax.experimental.pallas import tpu as pltpu
 from jax.sharding import PartitionSpec as P
+
 
 HD = 128
 EPS = 1e-06
@@ -253,28 +254,29 @@
     )(rows_attn, full_attn, full_attn, full_attn, *tables, *gains)
 
 
-def attend_back(rows_resid, full_out, out_column, saved, tables, gains, groups, per_group):
+def attend_back(
+    rows_resid, full_out, out_column, saved, tables, gains, groups, per_group, first, count
+):
     length, width = rows_resid.shape
     qraw, kraw, qb, kb, vb, lse = saved
     block = min(length, BLOCK)
-    heads = groups * per_group
-    columns = (heads + 2 * groups) * HD
+    columns = count * (per_group + 2) * HD
     whole = lambda shape: pl.BlockSpec(shape, lambda g: (0, 0))
-    wide = pl.BlockSpec((length, per_group * HD), lambda g: (0, g))
-    narrow = pl.BlockSpec((length, HD), lambda g: (0, g))
+    wide = pl.BlockSpec((length, per_group * HD), lambda g: (0, first + g))
+    narrow = pl.BlockSpec((length, HD), lambda g: (0, first + g))
     return pl.pallas_call(
-        functools.partial(attend_back_kernel, per_group=per_group, block=block, groups=groups),
+        functools.partial(attend_back_kernel, per_group=per_group, block=block, groups=count),
         name="attend_back",
-        grid=(groups,),
+        grid=(count,),
         in_specs=[
             whole((length, width)),
-            pl.BlockSpec((per_group * HD, width), lambda g: (g, out_column)),
+            pl.BlockSpec((per_group * HD, width), lambda g: (first + g, out_column)),
             wide,
             narrow,
             narrow,
             wide,
             narrow,
-            pl.BlockSpec((None, per_group, length), lambda g: (g, 0, 0)),
+            pl.BlockSpec((None, per_group, length), lambda g: (first + g, 0, 0)),
             whole((length, HD)),
             whole((length, HD)),
             whole((1, HD)),
@@ -287,9 +289,9 @@
         ],
         scratch_shapes=[pltpu.VMEM((length, HD), F32), pltpu.VMEM((length, HD), F32)],
         cost_estimate=pl.CostEstimate(
-            flops=2 * length * width * heads * HD + 7 * length * length * heads * HD,
+            flops=(2 * width + 7 * length) * length * count * per_group * HD,
             bytes_accessed=length * columns * 10,
-            transcendentals=length * length * heads,
+            transcendentals=length * length * count * per_group,
         ),
     )(rows_resid, full_out, qb, kb, vb, qraw, kraw, lse, *tables, *gains)
 
@@ -339,7 +341,7 @@
 
 def mlp(rows_x, rows_cot, part, parts, full_mlp, full_down, units, dtype, held=()):
     rows, width = rows_x.shape
-    block = next(b for b in (384, 256, 128) if units % b == 0)
+    block = next(b for b in (512, 384, 256, 128) if units % b == 0)
     steps = units // block
     whole = pl.BlockSpec((rows, width), lambda j: (0, 0))
     piece = pl.BlockSpec((rows, block), lambda j: (part, j))
@@ -381,6 +383,72 @@
     return value
 
 
+def pick(array, index, axis):
+    return lax.dynamic_index_in_dim(array, index, axis, keepdims=False)
+
+
+def near_stages(value, n_dp):
+    me = lax.axis_index("dp")
+    blocks = value.reshape(n_dp // 4, 2, 2, -1, value.shape[-1])
+    for bit, step, axis in ((me % 2, 1, 2), (me // 2 % 2, 2, 1)):
+        sent = pick(blocks, 1 - bit, axis)
+        got = yield (lax.ppermute(sent, "dp", [(i, i ^ step) for i in range(n_dp)]),)
+        blocks = pick(blocks, bit, axis) + got[0]
+    yield (blocks,)
+
+
+def line_stages(blocks, n_dp):
+    depth = n_dp // 4
+    level = lax.axis_index("dp") // 4
+    up = down = None
+    for step in range(1, depth):
+        send_up = pick(blocks, jnp.minimum(level + depth - step, depth - 1), 0)
+        send_down = pick(blocks, jnp.maximum(level - depth + step, 0), 0)
+        if step > 1:
+            send_up, send_down = send_up + up, send_down + down
+        up, down = yield (
+            lax.ppermute(send_up, "dp", [(i, i + 4) for i in range(4 * step)]),
+            lax.ppermute(send_down, "dp", [(i, i - 4) for i in range(n_dp - 4 * step, n_dp)]),
+        )
+    total = pick(blocks, level, 0).astype(F32)
+    if depth > 1:
+        total = total + up.astype(F32) + down.astype(F32)
+    yield (total,)
+
+
+def sum_stages(value, sizes):
+    for axis, size in sizes:
+        step = 1
+        while step < size:
+            got = yield (lax.ppermute(value, axis, [(i, i ^ step) for i in range(size)]),)
+            value = value + got[0]
+            step *= 2
+    yield (value,)
+
+
+class Waves:
+    def __init__(self, lengths):
+        self.lengths, self.chains, self.held, self.sums = lengths, {}, {}, {}
+
+    def add(self, name, chain):
+        self.chains[name] = chain
+        self.held[name] = next(chain)
+
+    def advance(self, *beside, only=None):
+        names = list(self.held) if only is None else [only]
+        values = [self.held.pop(n) for n in names]
+        if only is None:
+            values, beside = lax.optimization_barrier((values, beside))
+        for name, value in zip(names, values):
+            self.lengths[name] -= 1
+            got = self.chains[name].send(value)
+            if self.lengths[name]:
+                self.held[name] = got
+            else:
+                self.sums[name] = got[0]
+        return beside
+
+
 def pack_rows(shard, rows):
     count, width = shard.shape
     if 2 * count == 3 * rows and rows % 32 == 0:
@@ -486,14 +554,15 @@
         hidden_f = hidden_in.astype(F32)
         unit_attn, scale_attn = rms_unit(hidden_f)
         rows_hidden = sequence_rows(hidden_in)
-        rows_attn = (rms_unit(rows_hidden.astype(F32))[0] * gain_attention).astype(BF)
+        unit_rows = rms_unit(rows_hidden.astype(F32))[0]
+        rows_attn = (unit_rows * gain_attention).astype(BF)
+        if paired:
+            other_cot = swap(cotangent)
+            rows_attn, other_cot = lax.optimization_barrier((rows_attn, other_cot))
+        else:
+            rows_cot = lax.all_gather(cotangent, "tensor", axis=0, tiled=True)
         tables = rotary_tables(positions, HD)
         gains = (gain_query.reshape(1, HD), gain_key.reshape(1, HD))
-        if paired:
-            other_cot = swap(cotangent)
-        else:
-            rows_cot = lax.all_gather(cotangent, "tensor", axis=0, tiled=True)
-
         heads_b, *saved = attend(rows_attn, full_attn, tables, gains, groups_here, per_group)
         qraw, kraw, qb, kb, vb, lse = saved
         resid = hidden_f + scatter_rows(lambda h: matmul(h, full_out), heads_b)
@@ -541,39 +610,107 @@
         else:
             output_b = (resid + sum_rows(sent_down)).astype(BF)
 
-        grad_qkv_b, terms_qk = attend_back(
-            rows_resid,
-            out_source,
-            out_column,
-            (qraw, kraw, qb, kb, vb, lse),
-            tables,
-            gains,
-            groups_here,
-            per_group,
-        )
-        grad_attn_w = jnp.concatenate(
-            (
-                contract_rows(rows_attn, grad_qkv_b).astype(BF),
-                contract_rows(heads_b, rows_resid).astype(BF).reshape(width, -1),
-            ),
-            1,
-        )
-        grad_attn_w, sent_mlp = lax.optimization_barrier((grad_attn_w, sent_mlp))
-        sent_attn = lax.psum_scatter(grad_attn_w, "dp", scatter_dimension=0, tiled=True)
-        grad_normed_attn = scatter_rows(
-            lambda g: contract_cols(g, full_attn[:, :width_qkv]), grad_qkv_b
-        )
-        term_attention = jnp.sum(grad_normed_attn * unit_attn, 0)
+        back = functools.partial(
+            attend_back,
+            full_out=out_source,
+            out_column=out_column,
+            saved=(qraw, kraw, qb, kb, vb, lse),
+            tables=tables,
+            gains=gains,
+            groups=groups_here,
+            per_group=per_group,
+        )
+        wide, narrow = width_query // 2, width_key // 2
+        sizes = (("tensor", n_tensor), ("dp", n_dp))
+        if paired and n_dp % 4 == 0 and groups_here % 2 == 0 and n_dp & (n_dp - 1) == 0:
+            waves = Waves(
+                {"out": 2, "a": 2, "b": 2, "line": n_dp // 4 - 1, "terms": n_dp.bit_length()}
+            )
+            half = groups_here // 2
+            waves.add("out", near_stages(contract_rows(heads_b, rows_resid).astype(BF), n_dp))
+            grads_a, terms_a = back(rows_resid, first=0, count=half)
+            (rows_a,) = waves.advance(grads_a)
+            waves.add("a", near_stages(contract_rows(rows_attn, rows_a).astype(BF), n_dp))
+            grads_b, terms_b = back(rows_resid, first=half, count=half)
+            (rows_b,) = waves.advance(grads_b)
+            waves.add("b", near_stages(contract_rows(rows_attn, rows_b).astype(BF), n_dp))
+            waves.advance(only="b")
+
+            def part(g_a, g_b):
+                total = contract_cols(g_a[:, :wide], full_attn[:, :wide])
+                total += contract_cols(g_b[:, :wide], full_attn[:, wide:width_query])
+                for k in range(2):
+                    at = width_query + k * width_key
+                    to = wide + k * narrow
+                    total += contract_cols(
+                        g_a[:, to : to + narrow], full_attn[:, at : at + narrow]
+                    )
+                    total += contract_cols(
+                        g_b[:, to : to + narrow], full_attn[:, at + narrow : at + width_key]
+                    )
+                return total
+
+            me = lax.axis_index("tensor")
+            rows = rows_attn.shape[0] // 2
+
+            def take(array, index):
+                return lax.dynamic_slice_in_dim(array, index * rows, rows, 0)
+
+            other = part(take(rows_a, 1 - me), take(rows_b, 1 - me))
+            got = swap(other.astype(BF))
+            mine = part(take(rows_a, me), take(rows_b, me))
+            term_attention = jnp.sum(other * take(unit_rows, 1 - me), 0) + jnp.sum(
+                mine * unit_attn, 0
+            )
+            terms_qk = terms_a + terms_b
+            all_terms = jnp.concatenate(
+                (term_attention, term_feedforward, terms_qk[0], terms_qk[1])
+            ).reshape(-1, HD)
+            waves.add("terms", sum_stages(all_terms, sizes[::-1]))
+            waves.advance()
+            near = jnp.concatenate([waves.sums[n] for n in ("out", "a", "b")], -1)
+            waves.add("line", line_stages(near, n_dp))
+            while waves.held:
+                waves.advance()
+            grad_normed_attn = mine + got.astype(F32)
+            line, cut = waves.sums["line"], wide + 2 * narrow
+            sent_out, sent_a = line[:, :width], line[:, width : width + cut]
+            sent_b = line[:, width + cut :]
+            terms = waves.sums["terms"].reshape(-1)
+            sent_q = jnp.concatenate((sent_a[:, :wide], sent_b[:, :wide]), 1)
+            sent_k = jnp.concatenate(
+                (sent_a[:, wide : wide + narrow], sent_b[:, wide : wide + narrow]), 1
+            )
+            sent_v = jnp.concatenate((sent_a[:, wide + narrow :], sent_b[:, wide + narrow :]), 1)
+        else:
+            grad_qkv_b, terms_qk = back(rows_resid, first=0, count=groups_here)
+            grad_attn_w = jnp.concatenate(
+                (
+                    contract_rows(rows_attn, grad_qkv_b).astype(BF),
+                    contract_rows(heads_b, rows_resid).astype(BF).reshape(width, -1),
+                ),
+                1,
+            )
+            sent_attn = lax.psum_scatter(
+                grad_attn_w, "dp", scatter_dimension=0, tiled=True
+            ).astype(F32)
+            sent_q = sent_attn[:, :width_query]
+            sent_k = sent_attn[:, width_query : width_query + width_key]
+            sent_v = sent_attn[:, width_query + width_key : width_qkv]
+            sent_out = sent_attn[:, width_qkv:].reshape(out_proj.shape)
+            grad_normed_attn = scatter_rows(
+                lambda g: contract_cols(g, full_attn[:, :width_qkv]), grad_qkv_b
+            )
+            term_attention = jnp.sum(grad_normed_attn * unit_attn, 0)
+            terms = all_sum(
+                jnp.concatenate(
+                    (term_attention, term_feedforward, terms_qk[0], terms_qk[1])
+                ).reshape(-1, HD),
+                sizes,
+            ).reshape(-1)
         grad_hidden = grad_resid + rms_back(
             grad_normed_attn, gain_attention, unit_attn, scale_attn
         )
-        terms = all_sum(
-            jnp.concatenate(
-                (term_attention, term_feedforward, terms_qk[0], terms_qk[1])
-            ).reshape(-1, HD),
-            (("tensor", n_tensor), ("dp", n_dp)),
-        ).reshape(-1)
-        sent_attn = sent_attn.astype(F32)
         sent_mlp = sent_mlp.astype(F32)
         return (
             output_b,
@@ -582,10 +719,10 @@
             terms[width : 2 * width],
             terms[2 * width : 2 * width + HD],
             terms[2 * width + HD :],
-            sent_attn[:, :width_query],
-            sent_attn[:, width_query : width_query + width_key],
-            sent_attn[:, width_query + width_key : width_qkv],
-            sent_attn[:, width_qkv:].reshape(out_proj.shape),
+            sent_q,
+            sent_k,
+            sent_v,
+            sent_out,
             sent_mlp[:, :units],
             sent_mlp[:, units : 2 * units],
             unpack_rows(sent_mlp[:, 2 * units :], 1, width),
@@ -598,8 +735,10 @@
     rows = P(("dp", "tensor"), None)
     cut = P("dp", "tensor")
     stacked = P(("tensor", "dp"), None)
+    local = make_local(mesh.shape["dp"], mesh.shape["tensor"])
+
     return jax.shard_map(
-        make_local(mesh.shape["dp"], mesh.shape["tensor"]),
+        local,
         mesh=mesh,
         in_specs=(
             rows,

time: 451 us -> 425 us (0.942)
  waiting for transfers between devices: 226 us -> 170 us
  starting transfers between devices: 18.8 us -> 41.2 us
  other arithmetic: 33.2 us -> 39.2 us
    ppermute x8, waiting for transfers between devices: 135 us -> 108 us  [swap(): return lax.ppermute(value, 'tensor', [(0, 1), (1, 0)])]
    reduce_scatter x1 -> x0, waiting for transfers between devices: 23.9 us -> none  [local(): lax.psum_scatter(grad_attn_w, 'dp', scatter_dimension=0, tiled=True)]
    ppermute x5 -> x17, starting transfers between devices: 6.92 us -> 28.9 us  [the longest x3 15.2 us: line_stages(): lax.ppermute(send_up, 'dp', [(i, i + 4) for i in range(4 * step)])]
    ppermute x5 -> x17, waiting for transfers between devices: 5.87 us -> 27.6 us  [the longest x6 12.8 us: near_stages(): lax.ppermute(sent, 'dp', [(i, i ^ step) for i in range(n_dp)])]
    all_gather x1, waiting for transfers between devices: 31.9 us -> 13.3 us  [local(): full_attn = lax.all_gather(shard_attn, 'dp', axis=0, tiled=True)]
    reduce_scatter x1, waiting for transfers between devices: 9.05 us -> 0.01 us  [local(): lax.psum_scatter(grad_mlp_w, 'dp', scatter_dimension=0, tiled=True)]
    pallas_call x2, Pallas kernels: 39.2 us -> 33.9 us  [mlp(): pl.pallas_call(functools.partial(mlp_kernel, steps=steps), name='feed_for...]
    add x5 -> x16, other arithmetic: 0.03 us -> 5.24 us  [the longest x6 4.18 us: near_stages(): blocks = pick(blocks, bit, axis) + got[0]]
  transfers between devices with their start and end apart: 17 -> 28, of which waited for: 15 -> 13; matrix products, arithmetic and copies ran while one was open for 14% -> 18% of each run, Pallas kernels for 12% -> 14%
where the time goes in v3:
time: 425 us; the launch traced here: 420 us
  waiting for transfers between devices  170 us (40%)
  Pallas kernels  94.5 us (22%)
  matrix products  41.9 us (10%)
  starting transfers between devices  41.2 us (10%)
  other arithmetic  39.2 us (9%)
  local copies, waits for them, and re-layouts  18.7 us (4%)
  between operations  14.7 us (3%)
    ppermute x8, waiting for transfers between devices, swap(): return lax.ppermute(value, 'tensor', [(0, 1), (1, 0)])  108 us
    pallas_call x2, Pallas kernels, attend_back(): pl.pallas_call(functools.partial(attend_back_kernel, per_group=per_group,...  34.9 us
    pallas_call x2, Pallas kernels, mlp(): pl.pallas_call(functools.partial(mlp_kernel, steps=steps), name='feed_for...  33.9 us
    dot_general x6, matrix products, contract_rows(): lax.dot_general(left, right, (((0,), (0,)), ((), ())), preferred_element_...  26.9 us
    pallas_call x1, Pallas kernels, attend(): pl.pallas_call(functools.partial(attend_kernel, per_group=per_group, bloc...  25.7 us
    all_gather x1, waiting for transfers between devices, local(): full_mlp = lax.all_gather(shard_mlp, 'dp', axis=0, tiled=True)  20.7 us
    ppermute x3, starting transfers between devices, line_stages(): lax.ppermute(send_up, 'dp', [(i, i + 4) for i in range(4 * step)])  15.2 us
    all_gather x1, waiting for transfers between devices, local(): full_attn = lax.all_gather(shard_attn, 'dp', axis=0, tiled=True)  13.3 us
  transfers between devices with their start and end apart: 28, of which 13 were waited for; matrix products, arithmetic and copies ran while one was open for 18% of the time, Pallas kernels for 14%

profile of v3, /device:TPU:0, one launch (start us, length us, event | category | flops | bytes accessed | tf_op | source)
XLA Modules:
  0.0 420.4 jit_solution(11242120784926467006)
XLA Ops:
  7.3 1.9 pad_maximum_fusion.9
  11.0 1.9 maximum_maximum_fusion.2
  12.9 3.1 collective-permute-start
  16.1 1.9 fusion.59
  19.4 20.6 %collective-permute-done = bf16[512,1024]{1,0:T(8,128)(2,1)S(1)} collective-permute-done((bf16[512,1024]{1,0:T(8,128)(2,1)S(1)}, bf16[512,1024]{1,0:T(8,128)(2,1)S(1)}, u32[]{:S(2)}, u32[]{:S(2)}) %collective-permute-start) | collective-permute-done | bytes 1048608 | tf_op jit(solution)/shard_map/ppermute | solution.py:490
  40.8 3.4 convert_multiply_fusion
  44.2 17.5 %collective-permute-done.1.cot_ref = bf16[512,1024]{1,0:T(8,128)(2,1)} collective-permute-done((bf16[512,1024]{1,0:T(8,128)(2,1)S(1)}, bf16[512,1024]{1,0:T(8,128)(2,1)}, u32[]{:S(2)}, u32[]{:S(2)}) %collective-permute-start.1) | collective-permute-done | bytes 1048608 | tf_op jit(solution)/shard_map/ppermute | solution.py:490
  61.7 13.3 %all-gather.3.cloned.1.call-done.wq_ref.wk_ref.wv_ref.wo_ref = bf16[1024,3072]{1,0:T(8,128)(2,1)} async-done(((bf16[64,3072]{1,0:T(8,128)(2,1)}), bf16[1024,3072]{1,0:T(8,128)(2,1)}) %all-gather.3.cloned.1.call-update) | async-done | bytes 6291472 | tf_op jit(solution)/shard_map/all_gather | solution.py:544
  75.0 25.7 %attend.1 = (bf16[1024,1024]{1,0:T(8,128)(2,1)}, f32[1024,1024]{1,0:T(8,128)}, f32[1024,512]{1,0:T(8,128)}, bf16[1024,1024]{1,0:T(8,128)(2,1)}, bf16[1024,512]{1...) custom-call(bf16[1024,1024]{1,0:T(8,128)(2,1)} %get-tuple-element.55.x_ref, ...), custom_call_target="tpu_custom_call" | custom-call | flops 7516192768 | bytes 20971520 | tf_op jit(solution)/shard_map/attend/pallas_call | solution.py:217
  100.7 3.2 fusion.17
  103.9 1.5 collective-permute-start.2
  105.4 23.9 %collective-permute-done.2 = bf16[512,1024]{1,0:T(8,128)(2,1)} collective-permute-done((bf16[512,1024]{1,0:T(8,128)(2,1)S(1)}, bf16[512,1024]{1,0:T(8,128)(2,1)}, u32[]{:S(2)}, u32[]{:S(2)}) %collective-permute-start.2) | collective-permute-done | bytes 1048608 | tf_op jit(solution)/shard_map/ppermute | solution.py:490
  129.4 3.7 multiply_reduce_fusion.3
  136.2 20.7 %all-gather.5.cloned.1.call-done.wg_ref.wu_ref = bf16[1024,4608]{1,0:T(8,128)(2,1)} async-done(((bf16[64,4608]{1,0:T(8,128)(2,1)}), bf16[1024,4608]{1,0:T(8,128)(2,1)}) %all-gather.5.cloned.1.call-update) | async-done | bytes 9437200 | tf_op jit(solution)/shard_map/all_gather | solution.py:545
  156.9 2.1 slice.235
  159.4 2.0 maximum_maximum_fusion
  161.3 16.7 %feed_forward.2 = (bf16[1024,1536]{1,0:T(8,128)(2,1)}, bf16[1024,1536]{1,0:T(8,128)(2,1)}, bf16[1024,1536]{1,0:T(8,128)(2,1)}, bf16[512,1024]{1,0:T(8,128)(2,1)}, bf16[512,1024]{1,0:T(8,128)(2,1)}) custom-call(bf16[512,1024]{1,0:T(8,128)(2,1)} %collective-permute-done.3.x_ref, bf16[512,1024]{1,0:T(8,128)(2,1)} %collective-permute-done.1.cot_ref, ...), custom_call_target="tpu_custom_call" | custom-call | flops 9663676416 | bytes 14155776 | tf_op jit(solution)/shard_map/feed_forward/pallas_call | solution.py:350
  178.0 17.2 %feed_forward.3 = (bf16[1024,1536]{1,0:T(8,128)(2,1)}, bf16[1024,1536]{1,0:T(8,128)(2,1)}, bf16[1024,1536]{1,0:T(8,128)(2,1)}, f32[512,1024]{1,0:T(8,128)}, f32[512,1024]{1,0:T(8,128)}) custom-call(bf16[512,1024]{1,0:T(8,128)(2,1)} %multiply_convert_fusion.1.x_ref, ...), custom_call_target="tpu_custom_call", output_to_operand_aliasing={{0}: (5, {}), {1}: (6, {}), {2}: (7, {})} | custom-call | flops 9663676416 | bytes 14155776 | tf_op jit(solution)/shard_map/feed_forward/pallas_call | solution.py:350
  195.3 6.1 %convolution_convert_fusion = bf16[1536,1024]{1,0:T(8,128)(2,1)S(1)} fusion(bf16[1024,1536]{1,0:T(8,128)(2,1)} %get-tuple-element.67, bf16[512,1024]{1,0:T(8,128)(2,1)} %collective-permute-done.1.cot_ref, bf16[512,1024]{1,0:T(8,128)(2,1)} %cot_ref.1), kind=kOutput, calls=%fused_computation.5 | convolution fusion | flops 3226992640 | bytes 8388608 | tf_op jit(solution)/shard_map/dot_general | solution.py:45
  201.4 1.5 collective-permute-start.4
  202.9 5.7 %convolution_convert_fusion.2 = bf16[1024,1536]{1,0:T(8,128)(2,1)S(1)} fusion(bf16[1024,1536]{1,0:T(8,128)(2,1)S(1)} %copy-done.22, bf16[512,1024]{1,0:T(8,128)(2,1)} %collective-permute-done.3.x_ref, bf16[512,1024]{1,0:T(8,128)(2,1)} %multiply_convert_fusion.1.x_ref), kind=kOutput, calls=%fused_computation.7 | convolution fusion | flops 3226992640 | bytes 8388608 | tf_op jit(solution)/shard_map/dot_general | solution.py:45
  210.6 5.5 %convolution_convert_fusion.1 = bf16[1024,1536]{1,0:T(8,128)(2,1)S(1)} fusion(bf16[1024,1536]{1,0:T(8,128)(2,1)S(1)} %copy-done.23, bf16[512,1024]{1,0:T(8,128)(2,1)} %collective-permute-done.3.x_ref, bf16[512,1024]{1,0:T(8,128)(2,1)} %multiply_convert_fusion.1.x_ref), kind=kOutput, calls=%fused_computation.6 | convolution fusion | flops 3226992640 | bytes 8388608 | tf_op jit(solution)/shard_map/dot_general | solution.py:45
  216.1 10.7 %collective-permute-done.4 = bf16[512,1024]{1,0:T(8,128)(2,1)S(1)} collective-permute-done((bf16[512,1024]{1,0:T(8,128)(2,1)S(1)}, bf16[512,1024]{1,0:T(8,128)(2,1)S(1)}, u32[]{:S(2)}, u32[]{:S(2)}) %collective-permute-start.4) | collective-permute-done | bytes 1048608 | tf_op jit(solution)/shard_map/ppermute | solution.py:490
  228.0 2.4 fusion.70
  232.2 5.2 %pad_maximum_fusion = bf16[1024,4608]{1,0:T(8,128)(2,1)} fusion(bf16[1024,1536]{1,0:T(8,128)(2,1)S(1)} %bitcast.93, bf16[1024,1536]{1,0:T(8,128)(2,1)S(1)} %convolution_convert_fusion.1, bf16[1024,1536]{1,0:T(8,128)(2,1)S(1)} %convolution_convert_fusion.2), kind=kLoop, calls=%fused_computation | loop fusion | flops 28311552 | bytes 18874368 | tf_op jit(solution)/shard_map/concatenate | solution.py:590
  237.4 17.7 %collective-permute-done.5 = bf16[512,1024]{1,0:T(8,128)(2,1)S(1)} collective-permute-done((bf16[512,1024]{1,0:T(8,128)(2,1)}, bf16[512,1024]{1,0:T(8,128)(2,1)S(1)}, u32[]{:S(2)}, u32[]{:S(2)}) %collective-permute-start.5) | collective-permute-done | bytes 1048608 | tf_op jit(solution)/shard_map/ppermute | solution.py:490
  256.8 2.2 copy-done.24
  259.0 2.4 convolution_convert_fusion.5
  263.8 1.5 collective-permute-start.6
  265.4 17.8 %attend_back.3 = (bf16[1024,1024]{1,0:T(8,128)(2,1)}, f32[8,128]{1,0:T(8,128)}) custom-call(bf16[1024,1024]{1,0:T(8,128)(2,1)} %copy-done.2, bf16[1024,3072]{1,0:T(8,128)(2,1)} %all-gather.3.cloned.1.call-done.wq_ref.wk_ref.wv_ref.wo_ref, bf16[1024,1024]{1,0:T(8,128)(2,1)} %get-tuple-element.70.qb_ref, bf16[1024,512]{1,0:T(8,128)(2,1)} %get-tuple-element.71.kb_ref, ...), custom_call_target="tpu_custom_call" | custom-call | flops 4831838208 | bytes 10485760 | tf_op jit(solution)/shard_map/attend_back/pallas_call | solution.py:267
  283.1 17.2 %attend_back.2 = (bf16[1024,1024]{1,0:T(8,128)(2,1)}, f32[8,128]{1,0:T(8,128)}) custom-call(bf16[1024,1024]{1,0:T(8,128)(2,1)} %copy-done.2, bf16[1024,3072]{1,0:T(8,128)(2,1)} %all-gather.3.cloned.1.call-done.wq_ref.wk_ref.wv_ref.wo_ref, bf16[1024,1024]{1,0:T(8,128)(2,1)} %get-tuple-element.70.qb_ref, bf16[1024,512]{1,0:T(8,128)(2,1)} %get-tuple-element.71.kb_ref, ...), custom_call_target="tpu_custom_call" | custom-call | flops 4831838208 | bytes 10485760 | tf_op jit(solution)/shard_map/attend_back/pallas_call | solution.py:267
  301.0 4.8 %convolution_convert_fusion.4 = bf16[1024,1024]{1,0:T(8,128)(2,1)S(1)} fusion(bf16[1024,1024]{1,0:T(8,128)(2,1)} %get-tuple-element.55.x_ref, bf16[1024,1024]{1,0:T(8,128)(2,1)} %get-tuple-element.77), kind=kOutput, calls=%fused_computation.40 | convolution fusion | flops 2148532224 | bytes 6291456 | tf_op jit(solution)/shard_map/dot_general | solution.py:45
  312.6 12.8 %collective-permute-done.8 = bf16[4,64,1024]{2,1,0:T(8,128)(2,1)S(1)} collective-permute-done((bf16[4,64,1024]{2,1,0:T(8,128)(2,1)S(1)}, bf16[4,64,1024]{2,1,0:T(8,128)(2,1)S(1)}, u32[]{:S(2)}, u32[]{:S(2)}) %collective-permute-start.8) | collective-permute-done | bytes 524320 | tf_op jit(solution)/shard_map/ppermute | solution.py:395
  326.4 2.4 convolution_convert_fusion.3
  332.9 1.5 collective-permute-start.10
  339.1 1.5 collective-permute-start.13
  340.7 17.9 %collective-permute-done.10 = bf16[512,1024]{1,0:T(8,128)(2,1)S(1)} collective-permute-done((bf16[512,1024]{1,0:T(8,128)(2,1)S(1)}, bf16[512,1024]{1,0:T(8,128)(2,1)S(1)}, u32[]{:S(2)}, u32[]{:S(2)}) %collective-permute-start.10) | collective-permute-done | bytes 1048608 | tf_op jit(solution)/shard_map/ppermute | solution.py:490
  361.7 2.2 collective-permute-start.16
  365.6 2.8 add_convert_fusion
  368.5 4.1 collective-permute-done.16
  372.7 4.4 %collective-permute-start.19 = (bf16[64,3072]{1,0:T(8,128)(2,1)S(1)}, bf16[64,3072]{1,0:T(8,128)(2,1)S(1)}, u32[]{:S(2)}, u32[]{:S(2)}) collective-permute-start(bf16[64,3072]{1,0:T(8,128)(2,1)S(1)} %get-tuple-element.118), channel_id=1, source_target_pairs={{0,8},{2,10},{4,12},{6,14},{8,16},{10,18},{12,20},{14,22},{1,9},{3... | collective-permute-start | bytes 1179656 | tf_op jit(solution)/shard_map/ppermute | solution.py:410
  377.8 3.4 collective-permute-start.18
  381.3 3.9 collective-permute-done.18
  385.3 8.6 %collective-permute-start.22 = (bf16[64,3072]{1,0:T(8,128)(2,1)S(1)}, bf16[64,3072]{1,0:T(8,128)(2,1)S(1)}, u32[]{:S(2)}, u32[]{:S(2)}) collective-permute-start(bf16[64,3072]{1,0:T(8,128)(2,1)S(1)} %get-tuple-element.116), channel_id=1, source_target_pairs={{0,8},{2,10},{4,12},{6,14},{8,16},{10,18},{12,20},{14,22},{16,24},... | collective-permute-start | bytes 1179656 | tf_op jit(solution)/shard_map/ppermute | solution.py:410
  395.2 2.1 collective-permute-start.21
  397.3 2.0 fusion.7
  399.3 5.7 %collective-permute-done.21 = f32[18,128]{1,0:T(8,128)S(1)} collective-permute-done((f32[18,128]{1,0:T(8,128)S(1)}, f32[18,128]{1,0:T(8,128)S(1)}, u32[]{:S(2)}, u32[]{:S(2)}) %collective-permute-start.21) | collective-permute-done | bytes 9248 | tf_op jit(solution)/shard_map/ppermute | solution.py:423
  404.9 1.5 collective-permute-start.24
  (163 shorter events, 47.7 us)
Async XLA Ops:
  7.2 5.7 %copy-start.3 = (bf16[512,1024]{1,0:T(8,128)(2,1)S(1)}, bf16[512,1024]{1,0:T(8,128)(2,1)}, u32[]{:S(2)}) copy-start(bf16[512,1024]{1,0:T(8,128)(2,1)} %param.14) | copy-start | bytes 3145732
  7.2 8.8 %copy-start.15 = (bf16[512,1024]{1,0:T(8,128)(2,1)S(1)}, bf16[512,1024]{1,0:T(8,128)(2,1)}, u32[]{:S(2)}) copy-start(bf16[512,1024]{1,0:T(8,128)(2,1)} %cot_ref.1) | copy-start | bytes 3145732
  7.2 8.9 %copy-start.20 = (s32[1024]{0:T(1024)S(1)}, s32[1024]{0:T(1024)}, u32[]{:S(2)}) copy-start(s32[1024]{0:T(1024)} %param.15) | copy-start | bytes 12292
  7.2 67.8 %all-gather.3.cloned.1.call-start = ((), (), s32[]{:S(2)}) async-start(), calls=%async_computation.1 | async-start | bytes 6684672 | tf_op jit(solution)/shard_map/all_gather | solution.py:544
  9.2 147.7 %all-gather.5.cloned.1.call-start = ((), (), s32[]{:S(2)}) async-start(), calls=%async_computation.2 | async-start | bytes 10027008 | tf_op jit(solution)/shard_map/all_gather | solution.py:545
  12.9 397.7 %reduce-scatter.2.cloned.1.call-start = ((), (), s32[]{:S(2)}) async-start(), calls=%async_computation.3 | async-start | bytes 10027008 | tf_op jit(solution)/shard_map/reduce_scatter | solution.py:598
  12.9 27.1 %collective-permute-start = (bf16[512,1024]{1,0:T(8,128)(2,1)S(1)}, bf16[512,1024]{1,0:T(8,128)(2,1)S(1)}, u32[]{:S(2)}, u32[]{:S(2)}) collective-permute-start(bf16[512,1024]{1,0:T(8,128)(2,1)S(1)} %copy-done.3), channel_id=1, source_target_pairs={{0,1},{1,0},{2,3},{3,2},{4,5},{5,4},{6,7},{7,6},{8,9},{9,8},{10,11... | collective-permute-start | bytes 3145736 | tf_op jit(solution)/shard_map/ppermute | solution.py:490
  16.0 45.7 %collective-permute-start.1 = (bf16[512,1024]{1,0:T(8,128)(2,1)S(1)}, bf16[512,1024]{1,0:T(8,128)(2,1)}, u32[]{:S(2)}, u32[]{:S(2)}) collective-permute-start(bf16[512,1024]{1,0:T(8,128)(2,1)S(1)} %copy-done.15), channel_id=1, source_target_pairs={{0,1},{1,0},{2,3},{3,2},{4,5},{5,4},{6,7},{7,6},{8,9},{9,8},{10,11... | collective-permute-start | bytes 3145736 | tf_op jit(solution)/shard_map/ppermute | solution.py:490
  103.9 25.5 %collective-permute-start.2 = (bf16[512,1024]{1,0:T(8,128)(2,1)S(1)}, bf16[512,1024]{1,0:T(8,128)(2,1)}, u32[]{:S(2)}, u32[]{:S(2)}) collective-permute-start(bf16[512,1024]{1,0:T(8,128)(2,1)S(1)} %fusion.17), channel_id=1, source_target_pairs={{0,1},{1,0},{2,3},{3,2},{4,5},{5,4},{6,7},{7,6},{8,9},{9,8},{10,11... | collective-permute-start | bytes 3145736 | tf_op jit(solution)/shard_map/ppermute | solution.py:490
  105.4 27.6 %copy-start.18 = (f32[1024]{0:T(1024)S(1)}, f32[1024]{0:T(1024)}, u32[]{:S(2)}) copy-start(f32[1024]{0:T(1024)} %param.17) | copy-start | bytes 12292
  133.0 94.5 %copy-start = (f32[512,1024]{1,0:T(8,128)}, f32[512,1024]{1,0:T(8,128)S(1)}, u32[]{:S(2)}) copy-start(f32[512,1024]{1,0:T(8,128)S(1)} %get-tuple-element.143) | copy-start | bytes 6291460
  134.5 26.9 %collective-permute-start.3 = (bf16[512,1024]{1,0:T(8,128)(2,1)}, bf16[512,1024]{1,0:T(8,128)(2,1)}, u32[]{:S(2)}, u32[]{:S(2)}) collective-permute-start(bf16[512,1024]{1,0:T(8,128)(2,1)} %multiply_convert_fusion.1.x_ref), channel_id=1, source_target_pairs={{0,1},{1,0},{2,3},{3,2},{4,5},{5,4},{6,7},{7,6},{8,9},{9,8},{10,11... | collective-permute-start | bytes 3145736 | tf_op jit(solution)/shard_map/ppermute | solution.py:490
  195.3 6.1 %copy-start.21 = (bf16[512,1024]{1,0:T(8,128)(2,1)S(1)}, bf16[512,1024]{1,0:T(8,128)(2,1)}, u32[]{:S(2)}) copy-start(bf16[512,1024]{1,0:T(8,128)(2,1)} %get-tuple-element.63) | copy-start | bytes 3145732
  195.3 7.7 %copy-start.22 = (bf16[1024,1536]{1,0:T(8,128)(2,1)S(1)}, bf16[1024,1536]{1,0:T(8,128)(2,1)}, u32[]{:S(2)}) copy-start(bf16[1024,1536]{1,0:T(8,128)(2,1)} %get-tuple-element.65) | copy-start | bytes 9437188
  201.4 25.4 %collective-permute-start.4 = (bf16[512,1024]{1,0:T(8,128)(2,1)S(1)}, bf16[512,1024]{1,0:T(8,128)(2,1)S(1)}, u32[]{:S(2)}, u32[]{:S(2)}) collective-permute-start(bf16[512,1024]{1,0:T(8,128)(2,1)S(1)} %copy-done.21), channel_id=1, source_target_pairs={{0,1},{1,0},{2,3},{3,2},{4,5},{5,4},{6,7},{7,6},{8,9},{9,8},{10,11... | collective-permute-start | bytes 3145736 | tf_op jit(solution)/shard_map/ppermute | solution.py:490
  210.6 16.2 %copy-start.6 = (f32[512,1024]{1,0:T(8,128)S(1)}, f32[512,1024]{1,0:T(8,128)}, u32[]{:S(2)}) copy-start(f32[512,1024]{1,0:T(8,128)} %get-tuple-element.62) | copy-start | bytes 6291460
  230.4 24.7 %collective-permute-start.5 = (bf16[512,1024]{1,0:T(8,128)(2,1)}, bf16[512,1024]{1,0:T(8,128)(2,1)S(1)}, u32[]{:S(2)}, u32[]{:S(2)}) collective-permute-start(bf16[512,1024]{1,0:T(8,128)(2,1)} %get-tuple-element.101), channel_id=1, source_target_pairs={{0,1},{1,0},{2,3},{3,2},{4,5},{5,4},{6,7},{7,6},{8,9},{9,8},{10,11... | collective-permute-start | bytes 3145736 | tf_op jit(solution)/shard_map/ppermute | solution.py:490
  256.6 2.4 copy-start.24
  256.8 4.7 %copy-start.2 = (bf16[1024,1024]{1,0:T(8,128)(2,1)}, bf16[1024,1024]{1,0:T(8,128)(2,1)S(1)}, u32[]{:S(2)}) copy-start(bf16[1024,1024]{1,0:T(8,128)(2,1)S(1)} %pad_maximum_fusion.2.resid_ref) | copy-start | bytes 6291460
  263.8 37.2 %collective-permute-start.7 = (bf16[4,2,64,1024]{3,2,1,0:T(8,128)(2,1)}, bf16[4,2,64,1024]{3,2,1,0:T(8,128)(2,1)}, u32[]{:S(2)}, u32[]{:S(2)}) collective-permute-start(bf16[4,2,64,1024]{3,2,1,0:T(8,128)(2,1)} %dynamic-slice_bitcast_fusion.2), channel_id=1, source_target_pairs={{0,2},{2,0},{4,6},{6,4},{8,10},{10,8},{12,14},{14,12},{16,18},{18,... | collective-permute-start | bytes 3145736 | tf_op jit(solution)/shard_map/ppermute | solution.py:395
  263.8 101.8 %collective-permute-start.6 = (bf16[512,1024]{1,0:T(8,128)(2,1)}, bf16[512,1024]{1,0:T(8,128)(2,1)}, u32[]{:S(2)}, u32[]{:S(2)}) collective-permute-start(bf16[512,1024]{1,0:T(8,128)(2,1)} %get-tuple-element.68), channel_id=1, source_target_pairs={{0,1},{1,0},{2,3},{3,2},{4,5},{5,4},{6,7},{7,6},{8,9},{9,8},{10,11... | collective-permute-start | bytes 3145736 | tf_op jit(solution)/shard_map/ppermute | solution.py:490
  283.1 17.2 %copy-start.19 = (f32[8,128]{1,0:T(8,128)S(1)}, f32[8,128]{1,0:T(8,128)}, u32[]{:S(2)}) copy-start(f32[8,128]{1,0:T(8,128)} %get-tuple-element.82) | copy-start | bytes 12292
  283.1 26.0 %slice-start = ((s8[6291456]{0:T(1024)(128)(4,1)}), s8[2097152]{0:T(1024)(128)(4,1)S(1)}, s32[]{:S(2)}) async-start(s8[6291456]{0:T(1024)(128)(4,1)} %bitcast.91), calls=%async_computation.4 | async-start | bytes 4194304
  301.0 8.1 %slice-start.1 = ((s8[6291456]{0:T(1024)(128)(4,1)}), s8[4194304]{0:T(1024)(128)(4,1)S(1)}, s32[]{:S(2)}) async-start(s8[6291456]{0:T(1024)(128)(4,1)} %bitcast.91), calls=%async_computation.5 | async-start | bytes 8388608
  305.9 3.2 copy-start.13
  305.9 19.5 %collective-permute-start.9 = (bf16[4,2,64,1024]{3,2,1,0:T(8,128)(2,1)S(1)}, bf16[4,2,64,1024]{3,2,1,0:T(8,128)(2,1)S(1)}, u32[]{:S(2)}, u32[]{:S(2)}) collective-permute-start(bf16[4,2,64,1024]{3,2,1,0:T(8,128)(2,1)S(1)} %dynamic-slice_bitcast_fusion.1), channel_id=1, source_target_pairs={{0,2},{2,0},{4,6},{6,4},{8,10},{10,8},{12,14},{14,12},{16,18},{18,... | collective-permute-start | bytes 3145736 | tf_op jit(solution)/shard_map/ppermute | solution.py:395
  308.9 16.5 %collective-permute-start.8 = (bf16[4,64,1024]{2,1,0:T(8,128)(2,1)S(1)}, bf16[4,64,1024]{2,1,0:T(8,128)(2,1)S(1)}, u32[]{:S(2)}, u32[]{:S(2)}) collective-permute-start(bf16[4,64,1024]{2,1,0:T(8,128)(2,1)S(1)} %dynamic-slice_bitcast_fusion.5), channel_id=1, source_target_pairs={{0,4},{2,6},{4,0},{6,2},{8,12},{10,14},{12,8},{14,10},{16,20},{18,... | collective-permute-start | bytes 1572872 | tf_op jit(solution)/shard_map/ppermute | solution.py:395
  311.4 15.0 %copy-start.9 = (bf16[1024,1024]{1,0:T(8,128)(2,1)S(1)}, bf16[1024,1024]{1,0:T(8,128)(2,1)}, u32[]{:S(2)}) copy-start(bf16[1024,1024]{1,0:T(8,128)(2,1)} %get-tuple-element.55.x_ref) | copy-start | bytes 6291460
  311.8 14.6 %copy-start.8 = (bf16[1024,1024]{1,0:T(8,128)(2,1)S(1)}, bf16[1024,1024]{1,0:T(8,128)(2,1)}, u32[]{:S(2)}) copy-start(bf16[1024,1024]{1,0:T(8,128)(2,1)} %get-tuple-element.80) | copy-start | bytes 6291460
  329.9 7.8 %collective-permute-start.12 = (bf16[4,2,64,1024]{3,2,1,0:T(8,128)(2,1)}, bf16[4,2,64,1024]{3,2,1,0:T(8,128)(2,1)}, u32[]{:S(2)}, u32[]{:S(2)}) collective-permute-start(bf16[4,2,64,1024]{3,2,1,0:T(8,128)(2,1)} %dynamic-slice_bitcast_fusion), channel_id=1, source_target_pairs={{0,2},{2,0},{4,6},{6,4},{8,10},{10,8},{12,14},{14,12},{16,18},{18,... | collective-permute-start | bytes 3145736 | tf_op jit(solution)/shard_map/ppermute | solution.py:395
  329.9 2.2 copy-start.4
  332.9 25.6 %collective-permute-start.10 = (bf16[512,1024]{1,0:T(8,128)(2,1)S(1)}, bf16[512,1024]{1,0:T(8,128)(2,1)S(1)}, u32[]{:S(2)}, u32[]{:S(2)}) collective-permute-start(bf16[512,1024]{1,0:T(8,128)(2,1)S(1)} %get-tuple-element.110), channel_id=1, source_target_pairs={{0,1},{1,0},{2,3},{3,2},{4,5},{5,4},{6,7},{7,6},{8,9},{9,8},{10,11... | collective-permute-start | bytes 3145736 | tf_op jit(solution)/shard_map/ppermute | solution.py:490
  335.9 24.4 %collective-permute-start.11 = (bf16[4,64,1024]{2,1,0:T(8,128)(2,1)S(1)}, bf16[4,64,1024]{2,1,0:T(8,128)(2,1)S(1)}, u32[]{:S(2)}, u32[]{:S(2)}) collective-permute-start(bf16[4,64,1024]{2,1,0:T(8,128)(2,1)S(1)} %dynamic-slice_bitcast_fusion.4), channel_id=1, source_target_pairs={{0,4},{2,6},{4,0},{6,2},{8,12},{10,14},{12,8},{14,10},{16,20},{18,... | collective-permute-start | bytes 1572872 | tf_op jit(solution)/shard_map/ppermute | solution.py:395
  339.1 22.2 %collective-permute-start.13 = (bf16[4,64,1024]{2,1,0:T(8,128)(2,1)S(1)}, bf16[4,64,1024]{2,1,0:T(8,128)(2,1)S(1)}, u32[]{:S(2)}, u32[]{:S(2)}) collective-permute-start(bf16[4,64,1024]{2,1,0:T(8,128)(2,1)S(1)} %dynamic-slice_bitcast_fusion.3), channel_id=1, source_target_pairs={{0,4},{2,6},{4,0},{6,2},{8,12},{10,14},{12,8},{14,10},{16,20},{18,... | collective-permute-start | bytes 1572872 | tf_op jit(solution)/shard_map/ppermute | solution.py:395
  360.1 1.2 collective-permute-start.14
  361.5 4.2 copy-start.1
  361.5 4.2 copy-start.10
  361.7 10.9 %collective-permute-start.16 = (bf16[64,3072]{1,0:T(8,128)(2,1)S(1)}, bf16[64,3072]{1,0:T(8,128)(2,1)S(1)}, u32[]{:S(2)}, u32[]{:S(2)}) collective-permute-start(bf16[64,3072]{1,0:T(8,128)(2,1)S(1)} %get-tuple-element.120), channel_id=1, source_target_pairs={{0,8},{2,10},{4,12},{6,14},{1,9},{3,11},{5,13},{7,15}} | collective-permute-start | bytes 1179656 | tf_op jit(solution)/shard_map/ppermute | solution.py:410
  363.9 8.7 %collective-permute-start.17 = (bf16[64,3072]{1,0:T(8,128)(2,1)S(1)}, bf16[64,3072]{1,0:T(8,128)(2,1)S(1)}, u32[]{:S(2)}, u32[]{:S(2)}) collective-permute-start(bf16[64,3072]{1,0:T(8,128)(2,1)S(1)} %get-tuple-element.119), channel_id=1, source_target_pairs={{24,16},{26,18},{28,20},{30,22},{25,17},{27,19},{29,21},{31,23}} | collective-permute-start | bytes 1179656 | tf_op jit(solution)/shard_map/ppermute | solution.py:411
  364.6 3.8 collective-permute-start.15
  368.5 28.9 %copy-start.5 = (f32[512,1024]{1,0:T(8,128)S(1)}, f32[512,1024]{1,0:T(8,128)}, u32[]{:S(2)}) copy-start(f32[512,1024]{1,0:T(8,128)} %get-tuple-element.102) | copy-start | bytes 6291460
  372.7 12.5 %collective-permute-start.19 = (bf16[64,3072]{1,0:T(8,128)(2,1)S(1)}, bf16[64,3072]{1,0:T(8,128)(2,1)S(1)}, u32[]{:S(2)}, u32[]{:S(2)}) collective-permute-start(bf16[64,3072]{1,0:T(8,128)(2,1)S(1)} %get-tuple-element.118), channel_id=1, source_target_pairs={{0,8},{2,10},{4,12},{6,14},{8,16},{10,18},{12,20},{14,22},{1,9},{3... | collective-permute-start | bytes 1179656 | tf_op jit(solution)/shard_map/ppermute | solution.py:410
  377.1 8.1 %collective-permute-start.20 = (bf16[64,3072]{1,0:T(8,128)(2,1)S(1)}, bf16[64,3072]{1,0:T(8,128)(2,1)S(1)}, u32[]{:S(2)}, u32[]{:S(2)}) collective-permute-start(bf16[64,3072]{1,0:T(8,128)(2,1)S(1)} %get-tuple-element.117), channel_id=1, source_target_pairs={{16,8},{18,10},{20,12},{22,14},{24,16},{26,18},{28,20},{30,22},{17... | collective-permute-start | bytes 1179656 | tf_op jit(solution)/shard_map/ppermute | solution.py:411
  377.8 7.4 %collective-permute-start.18 = (f32[18,128]{1,0:T(8,128)S(1)}, f32[18,128]{1,0:T(8,128)S(1)}, u32[]{:S(2)}, u32[]{:S(2)}) collective-permute-start(f32[18,128]{1,0:T(8,128)S(1)} %fusion.87), channel_id=1, source_target_pairs={{0,8},{2,10},{4,12},{6,14},{8,0},{10,2},{12,4},{14,6},{16,24},{18,... | collective-permute-start | bytes 27656 | tf_op jit(solution)/shard_map/ppermute | solution.py:423
  385.3 19.6 %collective-permute-start.22 = (bf16[64,3072]{1,0:T(8,128)(2,1)S(1)}, bf16[64,3072]{1,0:T(8,128)(2,1)S(1)}, u32[]{:S(2)}, u32[]{:S(2)}) collective-permute-start(bf16[64,3072]{1,0:T(8,128)(2,1)S(1)} %get-tuple-element.116), channel_id=1, source_target_pairs={{0,8},{2,10},{4,12},{6,14},{8,16},{10,18},{12,20},{14,22},{16,24},... | collective-permute-start | bytes 1179656 | tf_op jit(solution)/shard_map/ppermute | solution.py:410
  393.9 11.1 %collective-permute-start.23 = (bf16[64,3072]{1,0:T(8,128)(2,1)S(1)}, bf16[64,3072]{1,0:T(8,128)(2,1)S(1)}, u32[]{:S(2)}, u32[]{:S(2)}) collective-permute-start(bf16[64,3072]{1,0:T(8,128)(2,1)S(1)} %get-tuple-element.115), channel_id=1, source_target_pairs={{8,0},{10,2},{12,4},{14,6},{16,8},{18,10},{20,12},{22,14},{24,16},... | collective-permute-start | bytes 1179656 | tf_op jit(solution)/shard_map/ppermute | solution.py:411
  395.2 9.8 %collective-permute-start.21 = (f32[18,128]{1,0:T(8,128)S(1)}, f32[18,128]{1,0:T(8,128)S(1)}, u32[]{:S(2)}, u32[]{:S(2)}) collective-permute-start(f32[18,128]{1,0:T(8,128)S(1)} %add.278), channel_id=1, source_target_pairs={{0,16},{2,18},{4,20},{6,22},{8,24},{10,26},{12,28},{14,30},{16,0},... | collective-permute-start | bytes 27656 | tf_op jit(solution)/shard_map/ppermute | solution.py:423
  404.9 4.5 %collective-permute-start.24 = (f32[18,128]{1,0:T(8,128)S(1)}, f32[18,128]{1,0:T(8,128)S(1)}, u32[]{:S(2)}, u32[]{:S(2)}) collective-permute-start(f32[18,128]{1,0:T(8,128)S(1)} %add.283), channel_id=1, source_target_pairs={{0,1},{1,0},{2,3},{3,2},{4,5},{5,4},{6,7},{7,6},{8,9},{9,8},{10,11... | collective-permute-start | bytes 27656 | tf_op jit(solution)/shard_map/ppermute | solution.py:423
  (7 other events, 9.9 us)
Sparse Core Ops, SparseCore 0:
  10.9 64.1 all-gather.2
  77.3 79.5 all-gather.4
  237.5 113.2 reduce-scatter.1
